TPU v7x, 256 devices: a whole 4x4x8 slice. The times are simulated.
256 devices in a mesh: fsdp: 16 (over y_lo, z), dp: 16 (over x, y_hi, core).
Axes of the slice: x: 4, y: 4 (y_hi: 2, y_lo: 2; y = y_hi * 2 + y_lo), z: 8, core: 2. Of those that a mesh axis runs over, the one named last changes fastest.
Arguments:
- patch_acts: bfloat16 [32768, 12288], P(('fsdp', 'dp')), may hold values from -6 to 6
- patch_slot: int32 [32768], P(('fsdp', 'dp')), may hold values from 0 to 1024, as said below
- out_grads: bfloat16 [16384, 3072], P(('fsdp', 'dp')), may hold values from -6 to 6
- latent_weight: bfloat16 [12288, 3072], P('dp', 'fsdp'), may hold values from -0.0546875 to 0.0546875
- step_size: bfloat16 [1, 3072], P(None, 'fsdp')
Outputs:
- grad_acts: bfloat16 [32768, 12288], P(('fsdp', 'dp'))
- grad_weight: float32 [12288, 3072], P('dp', 'fsdp')
- grad_step: float32 [1, 3072], P(None, 'fsdp')
Inputs may be any that keep to these rules, and one draw needn't show every extreme that they name: `patch_slot`: within each fsdp index, the used patch rows of every image owner come first in its 128 slots and carry a packed row below 1024, the others carry 1024; each packed row of the fsdp index receives exactly one patch row; in every fsdp index some image owner has all 128 slots used.
All inputs are finite; a program needn't handle non-finite values.
Results may differ from a plain program's by a relative error of at most 0.0049.
Values may be sent and summed in bfloat16 or wider, within the bound.
No kernel may reach another device: no remote copies, remote signals or barrier semaphores. Data moves between devices by JAX's collectives and lax.ppermute only.
A program may use at most 128 MiB of HBM per device.

v0:
```python
import jax
import jax.numpy as jnp
from jax import lax
from jax.sharding import PartitionSpec as P

FF_W = 12288


top_level = 7.0
wobble = 0.9
two_pi = 6.283185307179586
inv_root_two = 0.7071067811865476
inv_root_tau = 0.3989422804014327


def gelu_pair(values):
    normal_cdf = 0.5 * (1.0 + jax.scipy.special.erf(values * inv_root_two))
    density = jnp.exp(-0.5 * values * values) * inv_root_tau
    return (values * normal_cdf, normal_cdf + values * density)


def soft_quantize(weight, step):
    ratio = weight / step
    clipped = top_level * jnp.tanh(ratio / top_level)
    phase = two_pi * clipped
    quantized = clipped - wobble * jnp.sin(phase) / two_pi
    slope = (1.0 - wobble * jnp.cos(phase)) * (1.0 - clipped / top_level * (clipped / top_level))
    return (quantized, slope, ratio)


def contract_last(left, right):
    return lax.dot_general(
        left, right, (((1,), (1,)), ((), ())), preferred_element_type=jnp.float32
    )


def contract_first(left, right):
    return lax.dot_general(
        left, right, (((0,), (0,)), ((), ())), preferred_element_type=jnp.float32
    )


def shards(patch_acts, patch_slot, out_grads, latent_weight, step_size):
    dp_count = lax.axis_size("dp")
    capacity, features = patch_acts.shape
    hidden = features // dp_count
    packed_rows = out_grads.shape[0] * dp_count
    outgoing = patch_acts.reshape(capacity, dp_count, hidden)
    labels = jnp.broadcast_to(patch_slot[:, None], (capacity, dp_count))
    incoming, slot_labels = (
        lax.all_to_all(outgoing, "dp", split_axis=1, concat_axis=0, tiled=True),
        lax.all_to_all(labels, "dp", split_axis=1, concat_axis=0, tiled=True),
    )
    incoming = incoming.reshape(dp_count * capacity, hidden)
    slot_labels = slot_labels.reshape(dp_count * capacity)
    holder = jnp.zeros((packed_rows + 1, hidden), jnp.bfloat16).at[slot_labels].set(incoming)
    packed = holder[:packed_rows]
    act_full, gelu_slope = gelu_pair(packed.astype(jnp.float32))
    act = act_full.astype(jnp.bfloat16)
    full_grads = lax.all_gather(out_grads, "dp", axis=0, tiled=True)
    step_local = step_size.astype(jnp.float32)
    quantized, slope, ratio = soft_quantize(latent_weight.astype(jnp.float32), step_local)
    step_piece = lax.all_gather(step_size, "fsdp", axis=1, tiled=True).astype(jnp.float32)
    piece_quant, piece_slope, piece_ratio = soft_quantize(
        lax.all_gather(latent_weight, "fsdp", axis=1, tiled=True).astype(jnp.float32), step_piece
    )
    piece_weight = (step_piece * piece_quant).astype(jnp.bfloat16)
    columns = full_grads
    grad_hidden = contract_last(columns, piece_weight)
    grad_packed = (grad_hidden * gelu_slope).astype(jnp.bfloat16)
    padded = jnp.concatenate([grad_packed, jnp.zeros((1, hidden), jnp.bfloat16)], axis=0)
    picked = jnp.take(padded, slot_labels, axis=0).reshape(dp_count * capacity, 1, hidden)
    returned = lax.all_to_all(picked, "dp", split_axis=0, concat_axis=1, tiled=True)
    grad_acts = returned.reshape(capacity, features)
    columns = full_grads
    grad_qweight = lax.psum_scatter(
        contract_first(columns, act), "fsdp", scatter_dimension=0, tiled=True
    ).T
    grad_weight = grad_qweight * slope
    partial_step = jnp.sum(grad_qweight * (quantized - ratio * slope), axis=0, keepdims=True)
    scale_factor = (FF_W * top_level) ** (-0.5)
    grad_step = scale_factor * lax.psum(partial_step, "dp")
    return (grad_acts, grad_weight, grad_step)


def solution(mesh):
    return jax.shard_map(
        shards,
        mesh=mesh,
        in_specs=(
            P(("fsdp", "dp"), None),
            P(("fsdp", "dp")),
            P(("fsdp", "dp"), None),
            P("dp", "fsdp"),
            P(None, "fsdp"),
        ),
        out_specs=(P(("fsdp", "dp"), None), P("dp", "fsdp"), P(None, "fsdp")),
        check_vma=False,
    )
```

profile of v0, /device:TPU:1, one launch (start us, length us, event | category | flops | bytes accessed | tf_op | source)
XLA Modules:
  0.0 393.2 jit_solution(10012122353420767556)
XLA Ops:
  7.9 0.7 all-gather.3.cloned.1.call-update
  8.6 1.3 broadcast_in_dim.24
  9.9 8.4 %all-to-all-start = ((s32[128,16,1]{0,2,1:T(1,128)}), s32[128,16,1]{0,2,1:T(1,128)S(1)}, u32[]{:S(2)}, u32[]{:S(2)}) async-start(s32[128,16,1]{0,2,1:T(1,128)} %broadcast_in_dim.24), calls=%async_computation | async-start | bytes 16384 | tf_op jit(solution)/shard_map/all_to_all | solution.py:52
  18.4 3.5 copy.35
  21.8 2.8 copy.36
  25.3 6.6 %all-to-all-start.1 = ((bf16[128,16,768]{2,0,1:T(8,128)(2,1)}), bf16[128,16,768]{2,0,1:T(8,128)(2,1)S(1)}, u32[]{:S(2)}, u32[]{:S(2)}) async-start(bf16[128,16,768]{2,0,1:T(8,128)(2,1)} %copy.36), calls=%async_computation.1 | async-start | bytes 6291456 | tf_op jit(solution)/shard_map/all_to_all | solution.py:51
  31.9 46.8 %all-to-all-done.1 = bf16[128,16,768]{2,0,1:T(8,128)(2,1)S(1)} async-done(((bf16[128,16,768]{2,0,1:T(8,128)(2,1)}), bf16[128,16,768]{2,0,1:T(8,128)(2,1)S(1)}, u32[]{:S(2)}, u32[]{:S(2)}) %all-to-all-start.1) | async-done | bytes 3145760 | tf_op jit(solution)/shard_map/all_to_all | solution.py:51
  78.8 1.7 copy-done
  80.4 10.6 %scatter_custom_fusion = bf16[1025,768]{1,0:T(8,128)(2,1)S(1)} fusion(s32[2048]{0:T(1024)S(1)} %bitcast.43, bf16[2048,768]{1,0:T(8,128)(2,1)} %bitcast.41, bf16[]{:T(256)} %constant.16.clone.1), kind=kCustom, calls=%fused_computation.20 | custom fusion | bytes 1574912 | tf_op jit(solution)/shard_map/scatter | solution.py:56
  91.1 0.8 copy.47
  91.9 8.8 %all-gather.5.cloned.1.call-done = bf16[1024,3072]{1,0:T(8,128)(2,1)} async-done(((bf16[64,3072]{1,0:T(8,128)(2,1)}), bf16[1024,3072]{1,0:T(8,128)(2,1)}) %all-gather.5.cloned.1.call-update) | async-done | bytes 6291472 | tf_op jit(solution)/shard_map/all_gather | solution.py:60
  100.7 10.2 %convolution_bitcast_fusion = f32[3072,768]{0,1:T(8,128)} fusion(bf16[1024,3072]{1,0:T(8,128)(2,1)} %all-gather.5.cloned.1.call-done, bf16[1024,768]{0,1:T(8,128)(2,1)S(1)} %copy.47), kind=kOutput, calls=%fused_computation.8 | convolution fusion | flops 4836556800 | bytes 17301504 | tf_op jit(solution)/shard_map/dot_general | solution.py:38
  110.8 9.6 %copy.44 = f32[3072,768]{1,0:T(8,128)} copy(f32[3072,768]{0,1:T(8,128)} %convolution_bitcast_fusion) | data formatting | bytes 18874368
  122.7 32.8 %all-reduce.1 = bf16[3072]{0:T(1024)(128)(2,1)S(1)} all-reduce(bf16[3072]{0:T(1024)(128)(2,1)S(1)} %dynamic-update-slice), channel_id=1, replica_groups=mesh['fsdp'=16,'dp'=16] {'fsdp'}, use_global_device_ids=true, to_apply=%add.1 | all-reduce | flops 3072 | bytes 12288
  155.5 18.2 %all-gather.3.cloned.1.call-done = bf16[768,3072]{0,1:T(8,128)(2,1)} async-done(((bf16[768,192]{0,1:T(8,128)(2,1)}), bf16[768,3072]{0,1:T(8,128)(2,1)}) %all-gather.3.cloned.1.call-update) | async-done | bytes 4718608 | tf_op jit(solution)/shard_map/all_gather | solution.py:65
  173.7 44.4 %fusion.8 = bf16[1024,768]{0,1:T(8,128)(2,1)} fusion(bf16[1024,768]{0,1:T(8,128)(2,1)S(1)} %copy.47, bf16[1024,3072]{1,0:T(8,128)(2,1)} %all-gather.5.cloned.1.call-done, bf16[768,3072]{0,1:T(8,128)(2,1)} %all-gather.3.cloned.1.call-done, f32[3072]{0:T(1024)S(1)} %mul.123), kind=kOutput, calls=%fused_computation.17 | convolution fusion | flops 4861722624 | bytes 14168064 | tf_op jit(solution)/shard_map/dot_general | solution.py:32
  218.1 1.7 copy.48
  220.0 9.4 %gather_fusion = bf16[2048,768]{1,0:T(8,128)(2,1)} fusion(bf16[1025,768]{1,0:T(8,128)(2,1)S(1)} %concatenate.3.clone, s32[2048]{0:T(1024)S(1)} %broadcast_clamp_fusion), kind=kCustom, calls=%fused_computation | custom fusion | bytes 6299648 | tf_op jit(solution)/shard_map/jit(_take)/gather | solution.py:72
  229.4 2.1 bitcast_select_fusion
  232.0 3.7 reduce.2
  235.8 6.4 %reshape.124 = bf16[16,2,49152]{2,1,0:T(2,128)(2,1)} reshape(bf16[2048,768]{1,0:T(8,128)(2,1)} %reduce.2) | data formatting | bytes 6291456
  242.2 15.5 %all-to-all-start.2 = ((bf16[16,2,49152]{2,1,0:T(2,128)(2,1)}), bf16[16,2,49152]{2,1,0:T(2,128)(2,1)S(1)}, u32[]{:S(2)}, u32[]{:S(2)}) async-start(bf16[16,2,49152]{2,1,0:T(2,128)(2,1)} %reshape.124), calls=%async_computation.2 | async-start | bytes 6291456 | tf_op jit(solution)/shard_map/all_to_all | solution.py:73
  257.6 1.1 copy.41
  258.8 69.8 %all-to-all-done.2 = bf16[16,2,49152]{2,1,0:T(2,128)(2,1)S(1)} async-done(((bf16[16,2,49152]{2,1,0:T(2,128)(2,1)}), bf16[16,2,49152]{2,1,0:T(2,128)(2,1)S(1)}, u32[]{:S(2)}, u32[]{:S(2)}) %all-to-all-start.2) | async-done | bytes 3145760 | tf_op jit(solution)/shard_map/all_to_all | solution.py:73
  328.5 7.7 %reshape.125 = bf16[2048,1,768]{2,1,0:T(2,128)(2,1)} reshape(bf16[16,2,49152]{2,1,0:T(2,128)(2,1)S(1)} %all-to-all-done.2) | data formatting | bytes 6291456
  336.2 5.0 %copy.46 = bf16[2048,1,768]{2,0,1:T(8,128)(2,1)} copy(bf16[2048,1,768]{2,1,0:T(2,128)(2,1)} %reshape.125) | data formatting | bytes 6291456
  341.2 3.5 copy.40
  344.7 2.8 copy.42
  347.5 1.3 copy.45
  348.8 3.3 fusion.13
  352.1 1.1 copy.43
  353.2 32.9 %psum.7 = f32[1,192]{1,0:T(1,128)S(1)} all-reduce(f32[1,192]{1,0:T(1,128)S(1)} %bitcast.46), channel_id=1, replica_groups=mesh['fsdp'=16,'dp'=16] {'dp'}, use_global_device_ids=true, to_apply=%region_3.4 | all-reduce | flops 192 | bytes 1536 | tf_op jit(solution)/shard_map/psum | solution.py:82
  (24 shorter events, 4.3 us)
Async XLA Ops:
  7.2 93.5 %all-gather.5.cloned.1.call-start = ((), (), s32[]{:S(2)}) async-start(), calls=%async_computation.5 | async-start | bytes 6684672 | tf_op jit(solution)/shard_map/all_gather | solution.py:60
  7.9 165.8 %all-gather.3.cloned.1.call-start = ((), (), s32[]{:S(2)}) async-start(), calls=%async_computation.4 | async-start | bytes 5013504 | tf_op jit(solution)/shard_map/all_gather | solution.py:65
  9.9 15.4 %all-to-all-start = ((s32[128,16,1]{0,2,1:T(1,128)}), s32[128,16,1]{0,2,1:T(1,128)S(1)}, u32[]{:S(2)}, u32[]{:S(2)}) async-start(s32[128,16,1]{0,2,1:T(1,128)} %broadcast_in_dim.24), calls=%async_computation | async-start | bytes 16384 | tf_op jit(solution)/shard_map/all_to_all | solution.py:52
  25.3 53.5 %all-to-all-start.1 = ((bf16[128,16,768]{2,0,1:T(8,128)(2,1)}), bf16[128,16,768]{2,0,1:T(8,128)(2,1)S(1)}, u32[]{:S(2)}, u32[]{:S(2)}) async-start(bf16[128,16,768]{2,0,1:T(8,128)(2,1)} %copy.36), calls=%async_computation.1 | async-start | bytes 6291456 | tf_op jit(solution)/shard_map/all_to_all | solution.py:51
  31.8 315.6 %reduce-scatter.4.cloned.1.call-start = ((), (), s32[]{:S(2)}) async-start(), calls=%async_computation.6 | async-start | bytes 10027008
  78.8 1.7 copy-start
  120.5 0.7 copy-start.2
  120.5 1.9 copy-start.1
  242.2 86.4 %all-to-all-start.2 = ((bf16[16,2,49152]{2,1,0:T(2,128)(2,1)}), bf16[16,2,49152]{2,1,0:T(2,128)(2,1)S(1)}, u32[]{:S(2)}, u32[]{:S(2)}) async-start(bf16[16,2,49152]{2,1,0:T(2,128)(2,1)} %reshape.124), calls=%async_computation.2 | async-start | bytes 6291456 | tf_op jit(solution)/shard_map/all_to_all | solution.py:73
Sparse Core Ops, SparseCore 0:
  10.7 89.9 all-gather.4
  102.4 71.2 all-gather.2
  176.3 139.6 reduce-scatter.3
where the time goes:
time: 395 us; the launch traced here: 393 us
  waiting for transfers between devices  146 us (37%)
  local copies, waits for them, and re-layouts  72.3 us (18%)
  blocking collectives  65.7 us (17%)
  matrix products  54.6 us (14%)
  starting transfers between devices  30.6 us (8%)
  between operations  14.5 us (4%)
  other arithmetic  9.78 us (2%)
    all_to_all x1, waiting for transfers between devices, shards(): lax.all_to_all(picked, 'dp', split_axis=0, concat_axis=1, tiled=True)  69.8 us
    all_to_all x1, waiting for transfers between devices, shards(): lax.all_to_all(outgoing, 'dp', split_axis=1, concat_axis=0, tiled=True)  46.8 us
    dot_general x1, matrix products, contract_last(): lax.dot_general(left, right, (((1,), (1,)), ((), ())), preferred_element_...  44.4 us
    unnamed x20, local copies, waits for them, and re-layouts  44.1 us
    psum x1, blocking collectives, shards(): grad_step = scale_factor * lax.psum(partial_step, 'dp')  32.9 us
    unnamed x1, blocking collectives  32.8 us
    all_gather x1, waiting for transfers between devices, shards(): lax.all_gather(latent_weight, 'fsdp', axis=1, tiled=True)  18.2 us
    all_to_all x1, starting transfers between devices, shards(): lax.all_to_all(picked, 'dp', split_axis=0, concat_axis=1, tiled=True)  15.5 us
  transfers between devices with their start and end apart: 6, of which 5 were waited for; matrix products, arithmetic and copies ran while one was open for 33% of the time, Pallas kernels for 0%

commit v1 on v0

v1 whole, which is shorter than its diff:
```python
import functools

import jax
import jax.numpy as jnp
from jax import lax
from jax.experimental import pallas as pl
from jax.experimental.pallas import tpu as pltpu
from jax.sharding import Mesh, PartitionSpec as P

FF_W = 12288

top_level = 7.0
wobble = 0.9
two_pi = 6.283185307179586
inv_root_two = 0.7071067811865476
inv_root_tau = 0.3989422804014327

PARTS = ("a", "z", "x", "b", "c")
SIZES = (2, 8, 4, 2, 2)
FSDP = ("a", "z")
DP = ("x", "b", "c")
SWAP = [(0, 1), (1, 0)]

VMEM_LIMIT = 56 * 1024 * 1024


def gelu_pair(values):
    normal_cdf = 0.5 * (1.0 + lax.erf(values * inv_root_two))
    density = jnp.exp(-0.5 * values * values) * inv_root_tau
    return (values * normal_cdf, normal_cdf + values * density)


def soft_quantize(weight, step):
    ratio = weight / step
    clipped = top_level * jnp.tanh(ratio / top_level)
    phase = two_pi * clipped
    quantized = clipped - wobble * jnp.sin(phase) / two_pi
    slope = (1.0 - wobble * jnp.cos(phase)) * (1.0 - clipped / top_level * (clipped / top_level))
    return (quantized, slope, ratio)


def swap(value, axis):
    return lax.ppermute(value, axis, SWAP)


def shift(value, axis, by):
    count = lax.axis_size(axis)
    return lax.ppermute(value, axis, [(i, (i + by) % count) for i in range(count)])


def copy_block(source, target):
    target[...] = source[...].reshape(target.shape)


def split_columns(values, count):
    rows, width = values.shape[0], values.shape[1] // count
    return pl.pallas_call(
        copy_block,
        grid=(count,),
        in_specs=[pl.BlockSpec((rows, width), lambda i: (0, i))],
        out_specs=pl.BlockSpec((1, rows, width), lambda i: (i, 0, 0)),
        out_shape=jax.ShapeDtypeStruct((count, rows, width), values.dtype),
        name="split_columns",
    )(values)


def join_columns(values):
    count, rows, width = values.shape
    return pl.pallas_call(
        copy_block,
        grid=(count,),
        in_specs=[pl.BlockSpec((1, rows, width), lambda i: (i, 0, 0))],
        out_specs=pl.BlockSpec((rows, width), lambda i: (0, i)),
        out_shape=jax.ShapeDtypeStruct((rows, count * width), values.dtype),
        name="join_columns",
    )(values)


def weight_grad_body(place, incoming, grads, packed, out, act):
    rows = packed.shape[0]

    @pl.when(pl.program_id(0) == 0)
    def _():
        slots = incoming.shape[0]
        part = rows // 4
        for k in range(4):
            here = pl.ds(k * part, part)
            row = k * part + lax.broadcasted_iota(jnp.int32, (part, slots), 0)
            pick = (row == place[...]).astype(jnp.bfloat16)
            found = jnp.dot(pick, incoming[...], preferred_element_type=jnp.float32)
            packed[here, :] = found.astype(jnp.bfloat16)
            act[here, :] = gelu_pair(found)[0].astype(jnp.bfloat16)

    out[...] = lax.dot_general(
        grads[...], act[...], (((0,), (0,)), ((), ())), preferred_element_type=jnp.float32
    )


def weight_grad(place, incoming, grads):
    rows, outputs = grads.shape
    slots, hidden = incoming.shape
    tile = 384
    return pl.pallas_call(
        weight_grad_body,
        grid=(outputs // tile,),
        in_specs=[
            pl.BlockSpec((1, slots), lambda i: (0, 0)),
            pl.BlockSpec((slots, hidden), lambda i: (0, 0), pipeline_mode=pl.Buffered(1)),
            pl.BlockSpec((rows, tile), lambda i: (0, i)),
        ],
        out_specs=[
            pl.BlockSpec((rows, hidden), lambda i: (0, 0)),
            pl.BlockSpec((tile, hidden), lambda i: (i, 0)),
        ],
        out_shape=[
            jax.ShapeDtypeStruct((rows, hidden), jnp.bfloat16),
            jax.ShapeDtypeStruct((outputs, hidden), jnp.float32),
        ],
        scratch_shapes=[pltpu.VMEM((rows, hidden), jnp.bfloat16)],
        compiler_params=pltpu.CompilerParams(vmem_limit_bytes=VMEM_LIMIT),
        cost_estimate=pl.CostEstimate(
            flops=2 * rows * hidden * (outputs + slots),
            bytes_accessed=2 * rows * outputs + 4 * outputs * hidden + 2 * slots * hidden,
            transcendentals=rows * hidden,
        ),
        name="weight_grad",
    )(place, incoming, grads)


def hidden_grad_body(place, grads, weight, packed, out, pick):
    rows = packed.shape[0]
    slots = place.shape[0]

    @pl.when(pl.program_id(0) == 0)
    def _():
        column = lax.broadcasted_iota(jnp.int32, (slots, rows), 1)
        pick[...] = (column == place[...]).astype(jnp.bfloat16)

    grad = jnp.dot(grads[...], weight[...], preferred_element_type=jnp.float32)
    slope = gelu_pair(packed[...].astype(jnp.float32))[1]
    grad = (grad * slope).astype(jnp.bfloat16)
    found = jnp.dot(pick[...], grad, preferred_element_type=jnp.float32)
    out[...] = found.astype(jnp.bfloat16).reshape(out.shape)


def hidden_grad(place, grads, weight, packed, owners):
    rows, outputs = grads.shape
    hidden = packed.shape[1]
    slots = place.shape[0]
    tile = 256
    return pl.pallas_call(
        hidden_grad_body,
        grid=(hidden // tile,),
        in_specs=[
            pl.BlockSpec((slots, 1), lambda i: (0, 0), pipeline_mode=pl.Buffered(1)),
            pl.BlockSpec((rows, outputs), lambda i: (0, 0), pipeline_mode=pl.Buffered(1)),
            pl.BlockSpec((outputs, tile), lambda i: (0, i)),
            pl.BlockSpec((rows, tile), lambda i: (0, i)),
        ],
        out_specs=pl.BlockSpec((owners, slots // owners, tile), lambda i: (0, 0, i)),
        out_shape=jax.ShapeDtypeStruct((owners, slots // owners, hidden), jnp.bfloat16),
        scratch_shapes=[pltpu.VMEM((slots, rows), jnp.bfloat16)],
        compiler_params=pltpu.CompilerParams(vmem_limit_bytes=VMEM_LIMIT),
        cost_estimate=pl.CostEstimate(
            flops=2 * rows * hidden * (outputs + slots),
            bytes_accessed=2 * rows * outputs + 2 * outputs * hidden + 4 * slots * hidden,
            transcendentals=rows * hidden,
        ),
        name="hidden_grad",
    )(place, grads, weight, packed)


def gather_grads(own):
    half = own.shape[0]
    pair = jnp.concatenate([own, swap(own, "b")])
    above, below = shift(pair, "x", 1), shift(pair, "x", -1)
    pair_other = swap(pair, "c")
    far_first, far_second = shift(above[:half], "x", 1), shift(below[half:], "x", -1)
    above_other, below_other = swap(above, "c"), swap(below, "c")
    far_first_other, far_second_other = swap(far_first, "c"), swap(far_second, "c")
    return jnp.concatenate(
        [
            pair,
            pair_other,
            above,
            above_other,
            below,
            below_other,
            far_first,
            far_second,
            far_first_other,
            far_second_other,
        ]
    )


def places(slots, block):
    x, b, c = (lax.axis_index(name) for name in DP)
    owner = slots // block
    away = (owner // 4 - x) % 4
    turn = jnp.where(away == 0, 0, jnp.where(away == 3, 1, away + 1))
    other_b = (owner // 2 + b) % 2
    other_c = (owner + c) % 2
    where = ((turn * 2 + other_c) * 2 + other_b) * block + slots % block
    return jnp.where(slots < 16 * block, where, 32 * block)


def reduce_to_owner(partial):
    z, a = lax.axis_index("z"), lax.axis_index("a")
    _, count, width, hidden = partial.shape

    def own(turn, side=None):
        first, many = (0, 2) if side is None else (side, 1)
        piece = lax.dynamic_slice(
            partial, (first, (z + turn) % count, 0, 0), (many, 1, width, hidden)
        )[:, 0]
        return piece if side is None else piece[0]

    def narrow(value):
        return value.astype(jnp.bfloat16)

    def wide(value):
        return value.astype(jnp.float32)

    up = shift(narrow(own(4, 0)), "z", 1)
    down = shift(narrow(own(4, 1)), "z", -1)
    up = shift(jnp.stack([narrow(own(3, 0) + wide(up)), narrow(own(3, 1))]), "z", 1)
    down = shift(jnp.stack([narrow(own(-3, 0)), narrow(own(-3, 1) + wide(down))]), "z", -1)
    up = shift(narrow(own(2) + wide(up)), "z", 1)
    down = shift(narrow(own(-2) + wide(down)), "z", -1)
    up = shift(narrow(own(1) + wide(up)), "z", 1)
    down = shift(narrow(own(-1) + wide(down)), "z", -1)
    total = own(0) + wide(up) + wide(down)
    mine = lax.dynamic_index_in_dim(total, a, 0, False)
    other = lax.dynamic_index_in_dim(total, 1 - a, 0, False)
    return mine + wide(swap(narrow(other), "a"))


def shards(patch_acts, patch_slot, out_grads, latent_weight, step_size):
    capacity, features = patch_acts.shape
    block = out_grads.shape[0]
    hidden, width = latent_weight.shape

    step_column = step_size.astype(jnp.float32).reshape(width, 1)
    latent = latent_weight.T.astype(jnp.float32)
    quantized, slope, ratio = soft_quantize(latent, step_column)
    weight = lax.all_gather(
        (step_column * quantized).astype(jnp.bfloat16), FSDP, axis=0, tiled=True
    )
    slope, pull = lax.optimization_barrier((slope, quantized - ratio * slope))

    labels = jnp.broadcast_to(patch_slot[None, :], (16, capacity))
    labels = lax.all_to_all(labels, DP, split_axis=0, concat_axis=0, tiled=True)
    place = places(labels.reshape(16 * capacity), block)

    incoming = lax.all_to_all(
        split_columns(patch_acts, 16), DP, split_axis=0, concat_axis=0, tiled=True
    ).reshape(16 * capacity, hidden)
    grads = gather_grads(out_grads)

    packed, partial = weight_grad(place.reshape(1, -1), incoming, grads)
    grad_qweight = reduce_to_owner(partial.reshape(2, 8, width, hidden))

    picked = hidden_grad(place.reshape(-1, 1), grads, weight, packed, 16)
    returned = lax.all_to_all(picked, DP, split_axis=0, concat_axis=0, tiled=True)
    grad_acts = join_columns(returned)

    grad_weight = (grad_qweight * slope).T
    share = jnp.sum(grad_qweight * pull, axis=1)
    shares = lax.all_to_all(
        jnp.broadcast_to(share[None, :], (16, width)), DP, split_axis=0, concat_axis=0, tiled=True
    )
    scale_factor = (FF_W * top_level) ** (-0.5)
    grad_step = scale_factor * jnp.sum(shares, axis=0, keepdims=True)
    return (grad_acts, grad_weight, grad_step)


def solution(mesh):
    split = Mesh(mesh.devices.reshape(SIZES), PARTS)
    return jax.shard_map(
        shards,
        mesh=split,
        in_specs=(P(PARTS, None), P(PARTS), P(PARTS, None), P(DP, FSDP), P(None, FSDP)),
        out_specs=(P(PARTS, None), P(DP, FSDP), P(None, FSDP)),
        check_vma=False,
    )
```

time: 395 us -> 338 us (0.86)
  blocking collectives: 65.7 us -> 0 us
  Pallas kernels: 0 us -> 56.3 us
  matrix products: 54.6 us -> 0 us
  local copies, waits for them, and re-layouts: 72.3 us -> 24.7 us
  starting transfers between devices: 30.6 us -> 53.6 us
  waiting for transfers between devices: 146 us -> 163 us
  other arithmetic: 9.78 us -> 22 us
    ppermute x0 -> x19, waiting for transfers between devices: none -> 121 us  [the longest x12 114 us: shift(): lax.ppermute(value, axis, [(i, (i + by) % count) for i in range(count)])]
    all_to_all x3 -> x4, waiting for transfers between devices: 117 us -> 42.1 us  [the longest x1 39.2 us: shards(): lax.all_to_all(picked, DP, split_axis=0, concat_axis=0, tiled=True)]
    pallas_call x0 -> x4, Pallas kernels: none -> 56.3 us  [the longest x1 20.8 us: hidden_grad(): pl.pallas_call(hidden_grad_body, grid=(hidden // tile,), in_specs=[pl.Blo...]
    dot_general x2 -> x0, matrix products: 54.6 us -> none  [the longest x1 44.4 us: contract_last(): lax.dot_general(left, right, (((1,), (1,)), ((), ())), preferred_element_...]
    psum x1 -> x0, blocking collectives: 32.9 us -> none  [shards(): grad_step = scale_factor * lax.psum(partial_step, 'dp')]
    unnamed x1 -> x0, blocking collectives: 32.8 us -> none
    unnamed x20 -> x17, local copies, waits for them, and re-layouts: 44.1 us -> 16.9 us
    all_gather x2 -> x1, waiting for transfers between devices: 27 us -> 0.01 us  [shards(): lax.all_gather((step_column * quantized).astype(jnp.bfloat16), FSDP, axis...]
  transfers between devices with their start and end apart: 6 -> 24, of which waited for: 5 -> 10; matrix products, arithmetic and copies ran while one was open for 33% -> 13% of each run, Pallas kernels for 0% -> 14%
where the time goes in v1:
time: 338 us; the launch traced here: 334 us
  waiting for transfers between devices  163 us (48%)
  Pallas kernels  56.3 us (17%)
  starting transfers between devices  53.6 us (16%)
  local copies, waits for them, and re-layouts  24.7 us (7%)
  other arithmetic  22 us (7%)
  between operations  14.3 us (4%)
    ppermute x12, waiting for transfers between devices, shift(): lax.ppermute(value, axis, [(i, (i + by) % count) for i in range(count)])  114 us
    all_to_all x1, waiting for transfers between devices, shards(): lax.all_to_all(picked, DP, split_axis=0, concat_axis=0, tiled=True)  39.2 us
    pallas_call x1, Pallas kernels, hidden_grad(): pl.pallas_call(hidden_grad_body, grid=(hidden // tile,), in_specs=[pl.Blo...  20.8 us
    unnamed x17, local copies, waits for them, and re-layouts  16.9 us
    pallas_call x1, Pallas kernels, weight_grad(): pl.pallas_call(weight_grad_body, grid=(outputs // tile,), in_specs=[pl.Bl...  15.8 us
    ppermute x12, starting transfers between devices, shift(): lax.ppermute(value, axis, [(i, (i + by) % count) for i in range(count)])  14.5 us
    all_to_all x1, starting transfers between devices, shards(): lax.all_to_all(jnp.broadcast_to(share[None, :], (16, width)), DP, split_a...  10.9 us
    pallas_call x1, Pallas kernels, split_columns(): pl.pallas_call(copy_block, grid=(count,), in_specs=[pl.BlockSpec((rows, w...  9.81 us
  transfers between devices with their start and end apart: 24, of which 10 were waited for; matrix products, arithmetic and copies ran while one was open for 13% of the time, Pallas kernels for 14%

profile of v1, /device:TPU:1, one launch (start us, length us, event | category | flops | bytes accessed | tf_op | source)
XLA Modules:
  0.0 334.3 jit_solution(7066374432278561814)
XLA Ops:
  7.2 3.8 %collective-permute-start = (bf16[64,3072]{1,0:T(8,128)(2,1)}, bf16[64,3072]{1,0:T(8,128)(2,1)S(1)}, u32[]{:S(2)}, u32[]{:S(2)}) collective-permute-start(bf16[64,3072]{1,0:T(8,128)(2,1)} %param.7), channel_id=1, source_target_pairs={{0,2},{2,0},{1,3},{3,1},{4,6},{6,4},{5,7},{7,5},{8,10},{10,8},{9,1... | collective-permute-start | bytes 1179656 | tf_op jit(solution)/shard_map/ppermute | solution.py:43
  11.0 2.0 constant_dynamic-update-slice_fusion.1
  13.0 6.1 %collective-permute-done = bf16[64,3072]{1,0:T(8,128)(2,1)S(1)} collective-permute-done((bf16[64,3072]{1,0:T(8,128)(2,1)}, bf16[64,3072]{1,0:T(8,128)(2,1)S(1)}, u32[]{:S(2)}, u32[]{:S(2)}) %collective-permute-start) | collective-permute-done | bytes 393248 | tf_op jit(solution)/shard_map/ppermute | solution.py:43
  20.1 1.9 collective-permute-start.2
  23.2 2.3 collective-permute-start.1
  26.8 5.9 %all-to-all-start = ((s32[16,1,128]{2,1,0:T(1,128)}), s32[16,1,128]{2,1,0:T(1,128)S(1)}, u32[]{:S(2)}, u32[]{:S(2)}) async-start(s32[16,1,128]{2,1,0:T(1,128)} %broadcast_in_dim.22), calls=%async_computation | async-start | bytes 16384 | tf_op jit(solution)/shard_map/all_to_all | solution.py:253
  33.4 4.7 %fusion.25 = (f32[192,768]{1,0:T(8,128)}, f32[192,768]{1,0:T(8,128)}, bf16[192,768]{1,0:T(8,128)(2,1)}) fusion(f32[192]{0:T(256)S(1)} %bitcast.98, bf16[768,192]{0,1:T(8,128)(2,1)} %param.8), kind=kLoop, calls=%fused_computation.60 | loop fusion | flops 2359296 | bytes 1770240 | tf_op jit(solution)/shard_map/sub | solution.py:250
  38.1 9.8 %split_columns.1 = bf16[16,128,768]{2,1,0:T(8,128)(2,1)} custom-call(bf16[128,12288]{1,0:T(8,128)(2,1)} %source.1), custom_call_target="tpu_custom_call" | custom-call | tf_op jit(solution)/shard_map/split_columns/pallas_call | solution.py:57
  48.1 7.3 %all-to-all-start.1 = ((bf16[16,128,768]{2,1,0:T(8,128)(2,1)}), bf16[16,128,768]{2,1,0:T(8,128)(2,1)S(1)}, u32[]{:S(2)}, u32[]{:S(2)}) async-start(bf16[16,128,768]{2,1,0:T(8,128)(2,1)} %split_columns.1), calls=%async_computation.1 | async-start | bytes 6291456 | tf_op jit(solution)/shard_map/all_to_all | solution.py:256
  61.7 2.1 constant_dynamic-update-slice_fusion.10
  63.8 2.1 constant_dynamic-update-slice_fusion.9
  65.9 61.8 %collective-permute-done.6 = bf16[64,3072]{1,0:T(8,128)(2,1)S(1)} collective-permute-done((bf16[64,3072]{1,0:T(8,128)(2,1)S(1)}, bf16[64,3072]{1,0:T(8,128)(2,1)S(1)}, u32[]{:S(2)}, u32[]{:S(2)}) %collective-permute-start.6) | collective-permute-done | bytes 393248 | tf_op jit(solution)/shard_map/ppermute | solution.py:48
  128.3 2.1 constant_dynamic-update-slice_fusion.8
  130.4 2.1 constant_dynamic-update-slice_fusion.7
  136.5 2.9 all-to-all-done.1
  141.1 15.8 %weight_grad.1 = (bf16[1024,768]{1,0:T(8,128)(2,1)}, f32[3072,768]{1,0:T(8,128)}) custom-call(s32[1,2048]{1,0:T(1,128)} %compare_select_fusion.8.place, bf16[2048,768]{1,0:T(8,128)(2,1)} %bitcast.96, bf16[1024,3072]{1,0:T(8,128)(2,1)} %constant_dynamic-update-slice_fusion.2.grads), custom_call_target="tpu_custom_call" | custom-call | flops 8053063680 | bytes 18874368 | tf_op jit(solution)/shard_map/weight_grad/pallas_call | solution.py:103
  157.0 1.7 fusion.26
  158.8 2.9 collective-permute-start.14
  161.6 6.8 %collective-permute-done.10 = bf16[192,768]{1,0:T(8,128)(2,1)S(1)} collective-permute-done((bf16[192,768]{1,0:T(8,128)(2,1)S(1)}, bf16[192,768]{1,0:T(8,128)(2,1)S(1)}, u32[]{:S(2)}, u32[]{:S(2)}) %collective-permute-start.10) | collective-permute-done | bytes 294944 | tf_op jit(solution)/shard_map/ppermute | solution.py:48
  170.8 2.6 collective-permute-start.15
  173.5 11.4 %collective-permute-done.11 = bf16[2,192,768]{2,1,0:T(8,128)(2,1)S(1)} collective-permute-done((bf16[2,192,768]{2,1,0:T(8,128)(2,1)S(1)}, bf16[2,192,768]{2,1,0:T(8,128)(2,1)S(1)}, u32[]{:S(2)}, u32[]{:S(2)}) %collective-permute-start.11) | collective-permute-done | bytes 589856 | tf_op jit(solution)/shard_map/ppermute | solution.py:48
  186.4 13.9 %collective-permute-done.12 = bf16[2,192,768]{2,1,0:T(8,128)(2,1)S(1)} collective-permute-done((bf16[2,192,768]{2,1,0:T(8,128)(2,1)S(1)}, bf16[2,192,768]{2,1,0:T(8,128)(2,1)S(1)}, u32[]{:S(2)}, u32[]{:S(2)}) %collective-permute-start.12) | collective-permute-done | bytes 589856 | tf_op jit(solution)/shard_map/ppermute | solution.py:48
  200.4 2.8 fusion.3
  204.7 10.7 %collective-permute-done.16 = bf16[2,192,768]{2,1,0:T(8,128)(2,1)S(1)} collective-permute-done((bf16[2,192,768]{2,1,0:T(8,128)(2,1)}, bf16[2,192,768]{2,1,0:T(8,128)(2,1)S(1)}, u32[]{:S(2)}, u32[]{:S(2)}) %collective-permute-start.16) | collective-permute-done | bytes 589856 | tf_op jit(solution)/shard_map/ppermute | solution.py:48
  218.5 9.6 %collective-permute-done.17 = bf16[2,192,768]{2,1,0:T(8,128)(2,1)} collective-permute-done((bf16[2,192,768]{2,1,0:T(8,128)(2,1)S(1)}, bf16[2,192,768]{2,1,0:T(8,128)(2,1)}, u32[]{:S(2)}, u32[]{:S(2)}) %collective-permute-start.17) | collective-permute-done | bytes 589856 | tf_op jit(solution)/shard_map/ppermute | solution.py:48
  228.0 1.8 fusion.4
  230.2 4.5 %fusion.14.place = s32[2048,1]{1,0:T(8,128)} fusion(s32[2048,1]{1,0:T(8,128)S(1)} %copy.23, s32[]{:T(128)S(6)} %axis_index.58, s32[]{:T(128)S(6)} %axis_index.55, s32[]{:T(128)S(6)} %axis_index.53), kind=kLoop, calls=%fused_computation.40 | loop fusion | flops 190464 | bytes 16396 | tf_op jit(solution)/shard_map/jit(_where)/select_n | solution.py:205
  237.3 10.9 %all-to-all-start.3 = ((f32[16,1,192]{2,1,0:T(1,128)}), f32[16,1,192]{2,1,0:T(1,128)S(1)}, u32[]{:S(2)}, u32[]{:S(2)}) async-start(f32[16,1,192]{2,1,0:T(1,128)} %broadcast_in_dim.25), calls=%async_computation.3 | async-start | bytes 32768 | tf_op jit(solution)/shard_map/all_to_all | solution.py:270
  248.2 20.8 %hidden_grad.1 = bf16[16,128,768]{2,1,0:T(8,128)(2,1)} custom-call(s32[2048,1]{1,0:T(8,128)} %fusion.14.place, bf16[1024,3072]{1,0:T(8,128)(2,1)} %constant_dynamic-update-slice_fusion.2.grads, bf16[3072,768]{1,0:T(8,128)(2,1)} %all-gather.2.cloned.1.call-done.weight, bf16[1024,768]{1,0:T(8,128)(2,1)} %get-tuple-element.7.packed), custom_call_target="tpu_custom_call" | custom-call | flops 8053063680 | bytes 17301504 | tf_op jit(solution)/shard_map/hidden_grad/pallas_call | solution.py:151
  269.1 7.2 %all-to-all-start.2 = ((bf16[16,128,768]{2,1,0:T(8,128)(2,1)}), bf16[16,128,768]{2,1,0:T(8,128)(2,1)S(1)}, u32[]{:S(2)}, u32[]{:S(2)}) async-start(bf16[16,128,768]{2,1,0:T(8,128)(2,1)} %hidden_grad.1), calls=%async_computation.2 | async-start | bytes 6291456 | tf_op jit(solution)/shard_map/all_to_all | solution.py:265
  276.9 39.2 %all-to-all-done.2.source = bf16[16,128,768]{2,1,0:T(8,128)(2,1)S(1)} async-done(((bf16[16,128,768]{2,1,0:T(8,128)(2,1)}), bf16[16,128,768]{2,1,0:T(8,128)(2,1)S(1)}, u32[]{:S(2)}, u32[]{:S(2)}) %all-to-all-start.2) | async-done | bytes 3145760 | tf_op jit(solution)/shard_map/all_to_all | solution.py:265
  317.7 9.8 %join_columns.1 = bf16[128,12288]{1,0:T(8,128)(2,1)} custom-call(bf16[16,128,768]{2,1,0:T(8,128)(2,1)} %copy-done), custom_call_target="tpu_custom_call" | custom-call | tf_op jit(solution)/shard_map/join_columns/pallas_call | solution.py:69
  (61 shorter events, 30.8 us)
Async XLA Ops:
  7.2 11.9 %collective-permute-start = (bf16[64,3072]{1,0:T(8,128)(2,1)}, bf16[64,3072]{1,0:T(8,128)(2,1)S(1)}, u32[]{:S(2)}, u32[]{:S(2)}) collective-permute-start(bf16[64,3072]{1,0:T(8,128)(2,1)} %param.7), channel_id=1, source_target_pairs={{0,2},{2,0},{1,3},{3,1},{4,6},{6,4},{5,7},{7,5},{8,10},{10,8},{9,1... | collective-permute-start | bytes 1179656 | tf_op jit(solution)/shard_map/ppermute | solution.py:43
  20.1 27.9 %collective-permute-start.2 = (bf16[128,3072]{1,0:T(8,128)(2,1)}, bf16[128,3072]{1,0:T(8,128)(2,1)}, u32[]{:S(2)}, u32[]{:S(2)}) collective-permute-start(bf16[128,3072]{1,0:T(8,128)(2,1)} %get-tuple-element.21), channel_id=1, source_target_pairs={{0,4},{4,8},{8,12},{12,0},{1,5},{5,9},{9,13},{13,1},{2,6},{6,10},{... | collective-permute-start | bytes 2359304 | tf_op jit(solution)/shard_map/ppermute | solution.py:48
  22.0 36.7 %collective-permute-start.4 = (bf16[128,3072]{1,0:T(8,128)(2,1)}, bf16[128,3072]{1,0:T(8,128)(2,1)}, u32[]{:S(2)}, u32[]{:S(2)}) collective-permute-start(bf16[128,3072]{1,0:T(8,128)(2,1)} %get-tuple-element.21), channel_id=1, source_target_pairs={{0,12},{4,0},{8,4},{12,8},{1,13},{5,1},{9,5},{13,9},{2,14},{6,2},{... | collective-permute-start | bytes 2359304 | tf_op jit(solution)/shard_map/ppermute | solution.py:48
  23.2 38.5 %collective-permute-start.1 = (bf16[128,3072]{1,0:T(8,128)(2,1)}, bf16[128,3072]{1,0:T(8,128)(2,1)}, u32[]{:S(2)}, u32[]{:S(2)}) collective-permute-start(bf16[128,3072]{1,0:T(8,128)(2,1)} %get-tuple-element.21), channel_id=1, source_target_pairs={{0,1},{1,0},{2,3},{3,2},{4,5},{5,4},{6,7},{7,6},{8,9},{9,8},{10,11... | collective-permute-start | bytes 2359304 | tf_op jit(solution)/shard_map/ppermute | solution.py:43
  26.8 21.3 %all-to-all-start = ((s32[16,1,128]{2,1,0:T(1,128)}), s32[16,1,128]{2,1,0:T(1,128)S(1)}, u32[]{:S(2)}, u32[]{:S(2)}) async-start(s32[16,1,128]{2,1,0:T(1,128)} %broadcast_in_dim.22), calls=%async_computation | async-start | bytes 16384 | tf_op jit(solution)/shard_map/all_to_all | solution.py:253
  32.6 215.6 %all-gather.2.cloned.1.call-start = ((), (), s32[]{:S(2)}) async-start(), calls=%async_computation.4 | async-start | bytes 5013504 | tf_op jit(solution)/shard_map/all_gather | solution.py:247
  47.9 80.3 %collective-permute-start.3 = (bf16[128,3072]{1,0:T(8,128)(2,1)}, bf16[128,3072]{1,0:T(8,128)(2,1)}, u32[]{:S(2)}, u32[]{:S(2)}) collective-permute-start(bf16[128,3072]{1,0:T(8,128)(2,1)} %collective-permute-done.2), channel_id=1, source_target_pairs={{0,1},{1,0},{2,3},{3,2},{4,5},{5,4},{6,7},{7,6},{8,9},{9,8},{10,11... | collective-permute-start | bytes 2359304 | tf_op jit(solution)/shard_map/ppermute | solution.py:43
  48.1 91.4 %all-to-all-start.1 = ((bf16[16,128,768]{2,1,0:T(8,128)(2,1)}), bf16[16,128,768]{2,1,0:T(8,128)(2,1)S(1)}, u32[]{:S(2)}, u32[]{:S(2)}) async-start(bf16[16,128,768]{2,1,0:T(8,128)(2,1)} %split_columns.1), calls=%async_computation.1 | async-start | bytes 6291456 | tf_op jit(solution)/shard_map/all_to_all | solution.py:256
  57.2 70.5 %collective-permute-start.6 = (bf16[64,3072]{1,0:T(8,128)(2,1)S(1)}, bf16[64,3072]{1,0:T(8,128)(2,1)S(1)}, u32[]{:S(2)}, u32[]{:S(2)}) collective-permute-start(bf16[64,3072]{1,0:T(8,128)(2,1)S(1)} %slice.8), channel_id=1, source_target_pairs={{0,4},{4,8},{8,12},{12,0},{1,5},{5,9},{9,13},{13,1},{2,6},{6,10},{... | collective-permute-start | bytes 1179656 | tf_op jit(solution)/shard_map/ppermute | solution.py:48
  59.7 68.6 %collective-permute-start.7 = (bf16[64,3072]{1,0:T(8,128)(2,1)S(1)}, bf16[64,3072]{1,0:T(8,128)(2,1)S(1)}, u32[]{:S(2)}, u32[]{:S(2)}) collective-permute-start(bf16[64,3072]{1,0:T(8,128)(2,1)S(1)} %slice.9), channel_id=1, source_target_pairs={{0,12},{4,0},{8,4},{12,8},{1,13},{5,1},{9,5},{13,9},{2,14},{6,2},{... | collective-permute-start | bytes 1179656 | tf_op jit(solution)/shard_map/ppermute | solution.py:48
  61.1 71.4 %collective-permute-start.5 = (bf16[128,3072]{1,0:T(8,128)(2,1)}, bf16[128,3072]{1,0:T(8,128)(2,1)S(1)}, u32[]{:S(2)}, u32[]{:S(2)}) collective-permute-start(bf16[128,3072]{1,0:T(8,128)(2,1)} %collective-permute-done.4), channel_id=1, source_target_pairs={{0,1},{1,0},{2,3},{3,2},{4,5},{5,4},{6,7},{7,6},{8,9},{9,8},{10,11... | collective-permute-start | bytes 2359304 | tf_op jit(solution)/shard_map/ppermute | solution.py:43
  127.7 7.3 %collective-permute-start.8 = (bf16[64,3072]{1,0:T(8,128)(2,1)S(1)}, bf16[64,3072]{1,0:T(8,128)(2,1)S(1)}, u32[]{:S(2)}, u32[]{:S(2)}) collective-permute-start(bf16[64,3072]{1,0:T(8,128)(2,1)S(1)} %collective-permute-done.6), channel_id=1, source_target_pairs={{0,1},{1,0},{2,3},{3,2},{4,5},{5,4},{6,7},{7,6},{8,9},{9,8},{10,11... | collective-permute-start | bytes 1179656 | tf_op jit(solution)/shard_map/ppermute | solution.py:43
  128.3 7.5 %collective-permute-start.9 = (bf16[64,3072]{1,0:T(8,128)(2,1)S(1)}, bf16[64,3072]{1,0:T(8,128)(2,1)S(1)}, u32[]{:S(2)}, u32[]{:S(2)}) collective-permute-start(bf16[64,3072]{1,0:T(8,128)(2,1)S(1)} %collective-permute-done.7), channel_id=1, source_target_pairs={{0,1},{1,0},{2,3},{3,2},{4,5},{5,4},{6,7},{7,6},{8,9},{9,8},{10,11... | collective-permute-start | bytes 1179656 | tf_op jit(solution)/shard_map/ppermute | solution.py:43
  139.5 1.7 copy-start.1
  158.7 9.7 %collective-permute-start.10 = (bf16[192,768]{1,0:T(8,128)(2,1)S(1)}, bf16[192,768]{1,0:T(8,128)(2,1)S(1)}, u32[]{:S(2)}, u32[]{:S(2)}) collective-permute-start(bf16[192,768]{1,0:T(8,128)(2,1)S(1)} %get-tuple-element.15), channel_id=1, source_target_pairs={{0,16},{16,32},{32,48},{48,64},{64,80},{80,96},{96,112},{112,0},{1... | collective-permute-start | bytes 884744 | tf_op jit(solution)/shard_map/ppermute | solution.py:48
  158.8 9.6 %collective-permute-start.14 = (bf16[192,768]{1,0:T(8,128)(2,1)S(1)}, bf16[192,768]{1,0:T(8,128)(2,1)S(1)}, u32[]{:S(2)}, u32[]{:S(2)}) collective-permute-start(bf16[192,768]{1,0:T(8,128)(2,1)S(1)} %get-tuple-element.16), channel_id=1, source_target_pairs={{0,112},{16,0},{32,16},{48,32},{64,48},{80,64},{96,80},{112,96},{1... | collective-permute-start | bytes 884744 | tf_op jit(solution)/shard_map/ppermute | solution.py:48
  169.9 15.0 %collective-permute-start.11 = (bf16[2,192,768]{2,1,0:T(8,128)(2,1)S(1)}, bf16[2,192,768]{2,1,0:T(8,128)(2,1)S(1)}, u32[]{:S(2)}, u32[]{:S(2)}) collective-permute-start(bf16[2,192,768]{2,1,0:T(8,128)(2,1)S(1)} %pad_maximum_fusion), channel_id=1, source_target_pairs={{0,16},{16,32},{32,48},{48,64},{64,80},{80,96},{96,112},{112,0},{1... | collective-permute-start | bytes 1769480 | tf_op jit(solution)/shard_map/ppermute | solution.py:48
  170.8 15.6 %collective-permute-start.15 = (bf16[2,192,768]{2,1,0:T(8,128)(2,1)}, bf16[2,192,768]{2,1,0:T(8,128)(2,1)S(1)}, u32[]{:S(2)}, u32[]{:S(2)}) collective-permute-start(bf16[2,192,768]{2,1,0:T(8,128)(2,1)} %pad_maximum_fusion.1), channel_id=1, source_target_pairs={{0,112},{16,0},{32,16},{48,32},{64,48},{80,64},{96,80},{112,96},{1... | collective-permute-start | bytes 1769480 | tf_op jit(solution)/shard_map/ppermute | solution.py:48
  186.3 14.1 %collective-permute-start.12 = (bf16[2,192,768]{2,1,0:T(8,128)(2,1)S(1)}, bf16[2,192,768]{2,1,0:T(8,128)(2,1)S(1)}, u32[]{:S(2)}, u32[]{:S(2)}) collective-permute-start(bf16[2,192,768]{2,1,0:T(8,128)(2,1)S(1)} %fusion.2), channel_id=1, source_target_pairs={{0,16},{16,32},{32,48},{48,64},{64,80},{80,96},{96,112},{112,0},{1... | collective-permute-start | bytes 1769480 | tf_op jit(solution)/shard_map/ppermute | solution.py:48
  186.4 49.3 %copy-start.2 = (f32[192,768]{1,0:T(8,128)S(1)}, f32[192,768]{1,0:T(8,128)}, u32[]{:S(2)}) copy-start(f32[192,768]{1,0:T(8,128)} %get-tuple-element.10) | copy-start | bytes 1769476
  186.4 49.3 %copy-start.3 = (f32[192,768]{1,0:T(8,128)S(1)}, f32[192,768]{1,0:T(8,128)}, u32[]{:S(2)}) copy-start(f32[192,768]{1,0:T(8,128)} %get-tuple-element.9) | copy-start | bytes 1769476
  203.2 12.2 %collective-permute-start.16 = (bf16[2,192,768]{2,1,0:T(8,128)(2,1)}, bf16[2,192,768]{2,1,0:T(8,128)(2,1)S(1)}, u32[]{:S(2)}, u32[]{:S(2)}) collective-permute-start(bf16[2,192,768]{2,1,0:T(8,128)(2,1)} %get-tuple-element.12), channel_id=1, source_target_pairs={{0,112},{16,0},{32,16},{48,32},{64,48},{80,64},{96,80},{112,96},{1... | collective-permute-start | bytes 1769480 | tf_op jit(solution)/shard_map/ppermute | solution.py:48
  203.2 15.3 %collective-permute-start.13 = (bf16[2,192,768]{2,1,0:T(8,128)(2,1)S(1)}, bf16[2,192,768]{2,1,0:T(8,128)(2,1)}, u32[]{:S(2)}, u32[]{:S(2)}) collective-permute-start(bf16[2,192,768]{2,1,0:T(8,128)(2,1)S(1)} %get-tuple-element.11), channel_id=1, source_target_pairs={{0,16},{16,32},{32,48},{48,64},{64,80},{80,96},{96,112},{112,0},{1... | collective-permute-start | bytes 1769480 | tf_op jit(solution)/shard_map/ppermute | solution.py:48
  216.8 11.2 %collective-permute-start.17 = (bf16[2,192,768]{2,1,0:T(8,128)(2,1)S(1)}, bf16[2,192,768]{2,1,0:T(8,128)(2,1)}, u32[]{:S(2)}, u32[]{:S(2)}) collective-permute-start(bf16[2,192,768]{2,1,0:T(8,128)(2,1)S(1)} %fusion.1), channel_id=1, source_target_pairs={{0,112},{16,0},{32,16},{48,32},{64,48},{80,64},{96,80},{112,96},{1... | collective-permute-start | bytes 1769480 | tf_op jit(solution)/shard_map/ppermute | solution.py:48
  229.9 5.9 %collective-permute-start.18 = (bf16[192,768]{1,0:T(8,128)(2,1)S(1)}, bf16[192,768]{1,0:T(8,128)(2,1)S(1)}, u32[]{:S(2)}, u32[]{:S(2)}) collective-permute-start(bf16[192,768]{1,0:T(8,128)(2,1)S(1)} %fusion.30), channel_id=1, source_target_pairs={{0,128},{128,0},{1,129},{129,1},{2,130},{130,2},{3,131},{131,3},{4... | collective-permute-start | bytes 884744 | tf_op jit(solution)/shard_map/ppermute | solution.py:43
  237.3 31.8 %all-to-all-start.3 = ((f32[16,1,192]{2,1,0:T(1,128)}), f32[16,1,192]{2,1,0:T(1,128)S(1)}, u32[]{:S(2)}, u32[]{:S(2)}) async-start(f32[16,1,192]{2,1,0:T(1,128)} %broadcast_in_dim.25), calls=%async_computation.3 | async-start | bytes 32768 | tf_op jit(solution)/shard_map/all_to_all | solution.py:270
  269.1 47.0 %all-to-all-start.2 = ((bf16[16,128,768]{2,1,0:T(8,128)(2,1)}), bf16[16,128,768]{2,1,0:T(8,128)(2,1)S(1)}, u32[]{:S(2)}, u32[]{:S(2)}) async-start(bf16[16,128,768]{2,1,0:T(8,128)(2,1)} %hidden_grad.1), calls=%async_computation.2 | async-start | bytes 6291456 | tf_op jit(solution)/shard_map/all_to_all | solution.py:265
  316.0 1.6 copy-start
Sparse Core Ops, SparseCore 0:
  38.2 92.6 all-gather.1

commit v2 on v0

v2 whole, which is shorter than its diff:
```python
import functools

import jax
import jax.numpy as jnp
from jax import lax
from jax.experimental import pallas as pl
from jax.experimental.pallas import tpu as pltpu
from jax.sharding import Mesh, PartitionSpec as P

FF_W = 12288

top_level = 7.0
wobble = 0.9
two_pi = 6.283185307179586
inv_root_two = 0.7071067811865476
inv_root_tau = 0.3989422804014327

PARTS = ("a", "z", "x", "b", "c")
SIZES = (2, 8, 4, 2, 2)
FSDP = ("a", "z")
DP = ("x", "b", "c")
SWAP = [(0, 1), (1, 0)]

VMEM_LIMIT = 56 * 1024 * 1024


def gelu_pair(values):
    normal_cdf = 0.5 * (1.0 + lax.erf(values * inv_root_two))
    density = jnp.exp(-0.5 * values * values) * inv_root_tau
    return (values * normal_cdf, normal_cdf + values * density)


def soft_quantize(weight, step):
    ratio = weight / step
    clipped = top_level * jnp.tanh(ratio / top_level)
    phase = two_pi * clipped
    quantized = clipped - wobble * jnp.sin(phase) / two_pi
    slope = (1.0 - wobble * jnp.cos(phase)) * (1.0 - clipped / top_level * (clipped / top_level))
    return (quantized, slope, ratio)


def swap(value, axis):
    return lax.ppermute(value, axis, SWAP)


def shift(value, axis, by):
    count = lax.axis_size(axis)
    return lax.ppermute(value, axis, [(i, (i + by) % count) for i in range(count)])


def split_columns_body(width, source, codes, target):
    rows = source.shape[0]
    for k in range(target.shape[0]):
        target[k, :rows] = source[:, k * width : (k + 1) * width]
        target[k, rows:] = codes[...]


def split_columns(values, codes, count):
    rows, width = values.shape[0], values.shape[1] // count
    many = count // 2
    tall = rows + codes.shape[0]
    return pl.pallas_call(
        functools.partial(split_columns_body, width),
        grid=(count // many,),
        in_specs=[
            pl.BlockSpec((rows, many * width), lambda i: (0, i)),
            pl.BlockSpec(codes.shape, lambda i: (0, 0)),
        ],
        out_specs=pl.BlockSpec((many, tall, width), lambda i: (i, 0, 0)),
        out_shape=jax.ShapeDtypeStruct((count, tall, width), values.dtype),
        cost_estimate=pl.CostEstimate(
            flops=0, bytes_accessed=4 * values.size, transcendentals=0
        ),
        name="split_columns",
    )(values, codes)


def join_columns_body(width, source, target):
    for k in range(source.shape[0]):
        target[:, k * width : (k + 1) * width] = source[k]


def join_columns(values):
    count, rows, width = values.shape
    many = count // 2
    return pl.pallas_call(
        functools.partial(join_columns_body, width),
        grid=(count // many,),
        in_specs=[pl.BlockSpec((many, rows, width), lambda i: (i, 0, 0))],
        out_specs=pl.BlockSpec((rows, many * width), lambda i: (0, i)),
        out_shape=jax.ShapeDtypeStruct((rows, count * width), values.dtype),
        cost_estimate=pl.CostEstimate(
            flops=0, bytes_accessed=4 * values.size, transcendentals=0
        ),
        name="join_columns",
    )(values)


def stacked(pieces):
    return jnp.concatenate([piece[...] for piece in pieces])


def contract_rows(left, right):
    return lax.dot_general(
        left, right, (((0,), (0,)), ((), ())), preferred_element_type=jnp.float32
    )


def pack_body(place, incoming, packed, act):
    part, hidden = packed.shape
    slots = place.shape[1]
    row = pl.program_id(0) * part + lax.broadcasted_iota(jnp.int32, (part, slots), 0)
    pick = jnp.where(row == place[...], 1.0, 0.0).astype(jnp.bfloat16)
    source = incoming[...].reshape(slots, hidden)
    found = jnp.dot(pick, source, preferred_element_type=jnp.float32)
    packed[...] = found.astype(jnp.bfloat16)
    act[...] = gelu_pair(found)[0].astype(jnp.bfloat16)


def pack(place, incoming, rows):
    owners, _, hidden = incoming.shape
    slots = place.shape[1]
    steps = 4
    out = pl.BlockSpec((rows // steps, hidden), lambda i: (i, 0))
    return pl.pallas_call(
        pack_body,
        grid=(steps,),
        in_specs=[
            pl.BlockSpec((1, slots), lambda i: (0, 0)),
            pl.BlockSpec(
                (owners, slots // owners, hidden),
                lambda i: (0, 0, 0),
                pipeline_mode=pl.Buffered(1),
            ),
        ],
        out_specs=[out, out],
        out_shape=[jax.ShapeDtypeStruct((rows, hidden), jnp.bfloat16)] * 2,
        compiler_params=pltpu.CompilerParams(vmem_limit_bytes=VMEM_LIMIT),
        cost_estimate=pl.CostEstimate(
            flops=2 * rows * hidden * slots,
            bytes_accessed=2 * slots * hidden + 4 * rows * hidden,
            transcendentals=rows * hidden,
        ),
        name="pack",
    )(place, incoming)


def weight_grad_body(act, *refs):
    pieces, out = refs[:-1], refs[-1]
    grad = contract_rows(stacked(pieces), act[...])
    out[...] = narrow(grad).reshape(out.shape)


def weight_grad(act, pieces, count, sides, width):
    rows, hidden = act.shape
    outputs = pieces[0].shape[1]
    steps = 4
    tile = outputs // steps
    deep = tile // width
    around = count // deep
    return pl.pallas_call(
        weight_grad_body,
        grid=(steps,),
        in_specs=[pl.BlockSpec((rows, hidden), lambda i: (0, 0), pipeline_mode=pl.Buffered(1))]
        + [pl.BlockSpec((piece.shape[0], tile), lambda i: (0, i)) for piece in pieces],
        out_specs=pl.BlockSpec(
            (deep, 1, width, hidden), lambda i: (i % around, i // around, 0, 0)
        ),
        out_shape=jax.ShapeDtypeStruct((count, sides, width, hidden), jnp.bfloat16),
        compiler_params=pltpu.CompilerParams(vmem_limit_bytes=VMEM_LIMIT),
        cost_estimate=pl.CostEstimate(
            flops=2 * rows * hidden * outputs,
            bytes_accessed=2 * rows * (outputs + hidden) + 2 * outputs * hidden,
            transcendentals=0,
        ),
        name="weight_grad",
    )(act, *pieces)


def hidden_grad_body(weight, *refs):
    pieces, total = refs[:-1], refs[-1]
    step = pl.program_id(0)
    grads = stacked(pieces)
    block = weight[...].reshape(grads.shape[1], total.shape[1])
    grad = jnp.dot(grads, block, preferred_element_type=jnp.float32)

    @pl.when(step == 0)
    def _():
        total[...] = grad

    @pl.when(step > 0)
    def _():
        total[...] += grad


def hidden_grad(pieces, weight):
    rows = sum(piece.shape[0] for piece in pieces)
    outputs = pieces[0].shape[1]
    steps = 4
    tile = outputs // steps
    count, sides, width, hidden = weight.shape
    deep = tile // width
    around = count // deep
    return pl.pallas_call(
        hidden_grad_body,
        grid=(steps,),
        in_specs=[
            pl.BlockSpec((deep, 1, width, hidden), lambda i: (i % around, i // around, 0, 0)),
        ]
        + [pl.BlockSpec((piece.shape[0], tile), lambda i: (0, i)) for piece in pieces],
        out_specs=pl.BlockSpec((rows, hidden), lambda i: (0, 0)),
        out_shape=jax.ShapeDtypeStruct((rows, hidden), jnp.float32),
        compiler_params=pltpu.CompilerParams(vmem_limit_bytes=VMEM_LIMIT),
        cost_estimate=pl.CostEstimate(
            flops=2 * rows * hidden * outputs,
            bytes_accessed=2 * rows * outputs + 2 * outputs * hidden + 4 * rows * hidden,
            transcendentals=0,
        ),
        name="hidden_grad",
    )(weight, *pieces)


def unpack_body(place, packed, grad, out, final):
    rows = packed.shape[0]
    owners, each, hidden = out.shape
    slots = owners * each

    @pl.when(pl.program_id(0) == 0)
    def _():
        slope = gelu_pair(packed[...].astype(jnp.float32))[1]
        final[...] = (grad[...] * slope).astype(jnp.bfloat16)

    column = lax.broadcasted_iota(jnp.int32, (slots, rows), 1)
    pick = jnp.where(column == place[...], 1.0, 0.0).astype(jnp.bfloat16)
    found = jnp.dot(pick, final[...], preferred_element_type=jnp.float32)
    out[...] = found.astype(jnp.bfloat16).reshape(out.shape)


def unpack(place, packed, grad, owners):
    rows, hidden = packed.shape
    slots = place.shape[0]
    steps = 4
    return pl.pallas_call(
        unpack_body,
        grid=(steps,),
        in_specs=[
            pl.BlockSpec((slots // steps, 1), lambda i: (i, 0)),
            pl.BlockSpec((rows, hidden), lambda i: (0, 0), pipeline_mode=pl.Buffered(1)),
            pl.BlockSpec((rows, hidden), lambda i: (0, 0), pipeline_mode=pl.Buffered(1)),
        ],
        out_specs=pl.BlockSpec(
            (owners // steps, slots // owners, hidden), lambda i: (i, 0, 0)
        ),
        out_shape=jax.ShapeDtypeStruct((owners, slots // owners, hidden), jnp.bfloat16),
        scratch_shapes=[pltpu.VMEM((rows, hidden), jnp.bfloat16)],
        compiler_params=pltpu.CompilerParams(vmem_limit_bytes=VMEM_LIMIT),
        cost_estimate=pl.CostEstimate(
            flops=2 * rows * hidden * slots,
            bytes_accessed=2 * slots * hidden + 6 * rows * hidden,
            transcendentals=rows * hidden,
        ),
        name="unpack",
    )(place, packed, grad)


def gather_grads(own):
    half = own.shape[0]
    pair = jnp.concatenate([own, swap(own, "b")])
    above, below = shift(pair, "x", 1), shift(pair, "x", -1)
    pair_other = swap(pair, "c")
    far_first, far_second = shift(above[:half], "x", 1), shift(below[half:], "x", -1)
    above_other, below_other = swap(above, "c"), swap(below, "c")
    far_first_other, far_second_other = swap(far_first, "c"), swap(far_second, "c")
    return [
        pair,
        pair_other,
        above,
        above_other,
        below,
        below_other,
        far_first,
        far_second,
        far_first_other,
        far_second_other,
    ]


def places(slots, block):
    x, b, c = (lax.axis_index(name) for name in DP)
    owner = slots // block
    away = (owner // 4 - x) % 4
    turn = jnp.where(away == 0, 0, jnp.where(away == 3, 1, away + 1))
    other_b = (owner // 2 + b) % 2
    other_c = (owner + c) % 2
    where = ((turn * 2 + other_c) * 2 + other_b) * block + slots % block
    return jnp.where(slots < 16 * block, where, 32 * block)


def narrow(value):
    return value.astype(jnp.bfloat16)


def wide(value):
    return value.astype(jnp.float32)


def after(value, *others):
    return lax.optimization_barrier((value, *others))[0]


def shards(patch_acts, patch_slot, out_grads, latent_weight, step_size):
    capacity, features = patch_acts.shape
    block = out_grads.shape[0]
    hidden, width = latent_weight.shape

    pieces = gather_grads(out_grads)

    step_column = wide(step_size).reshape(width, 1)
    latent = wide(latent_weight.T)
    weight = narrow(step_column * soft_quantize(latent, step_column)[0])
    weight = lax.optimization_barrier(weight)
    other = after(swap(weight, "a"), pieces[0])
    first = lax.axis_index("a") == 0
    weight = jnp.stack([jnp.where(first, weight, other), jnp.where(first, other, weight)])
    weight = lax.all_gather(weight, "z", axis=0)

    codes = jnp.concatenate([patch_slot // 32, patch_slot % 32]).astype(jnp.bfloat16)
    codes = jnp.zeros((8, hidden), jnp.bfloat16).at[0, : 2 * capacity].set(codes)
    outgoing = after(split_columns(patch_acts, codes, 16), pieces[6], pieces[7])
    incoming = lax.all_to_all(outgoing, DP, split_axis=0, concat_axis=0, tiled=True)

    latent = wide(after(latent_weight, pieces[2]).T)
    quantized, slope, ratio = soft_quantize(latent, step_column)
    slope, pull = lax.optimization_barrier((slope, quantized - ratio * slope))
    grad = hidden_grad(pieces, weight)
    incoming, grad = lax.optimization_barrier((incoming, grad))

    codes = incoming[:, capacity, : 2 * capacity].astype(jnp.int32)
    slots = codes[:, :capacity] * 32 + codes[:, capacity:]
    place = places(slots.reshape(16 * capacity), block)
    packed, act = pack(place.reshape(1, -1), incoming, 16 * block)
    partial = weight_grad(act, pieces, 8, 2, width)
    packed = after(packed, partial)
    picked = unpack(after(place, act).reshape(-1, 1), packed, grad, 16)
    summed = lax.psum_scatter(partial, "z", scatter_dimension=0, tiled=True)[0]
    a = lax.axis_index("a")
    mine = lax.dynamic_index_in_dim(summed, a, 0, False)
    other = lax.dynamic_index_in_dim(summed, 1 - a, 0, False)
    grad_qweight = wide(mine) + wide(swap(other, "a"))

    returned = lax.all_to_all(picked, DP, split_axis=0, concat_axis=0, tiled=True)
    grad_acts = join_columns(returned)

    grad_weight = (grad_qweight * slope).T
    share = after(jnp.sum(grad_qweight * pull, axis=1), returned)
    shares = lax.all_to_all(
        jnp.broadcast_to(share[None, :], (16, width)), DP, split_axis=0, concat_axis=0, tiled=True
    )
    scale_factor = (FF_W * top_level) ** (-0.5)
    grad_step = scale_factor * jnp.sum(shares, axis=0, keepdims=True)
    return (grad_acts, grad_weight, grad_step)


def solution(mesh):
    split = Mesh(mesh.devices.reshape(SIZES), PARTS)
    return jax.shard_map(
        shards,
        mesh=split,
        in_specs=(P(PARTS, None), P(PARTS), P(PARTS, None), P(DP, FSDP), P(None, FSDP)),
        out_specs=(P(PARTS, None), P(DP, FSDP), P(None, FSDP)),
        check_vma=False,
    )
```

time: 395 us -> 228 us (0.58)
  local copies, waits for them, and re-layouts: 72.3 us -> 6.22 us
  blocking collectives: 65.7 us -> 0 us
  matrix products: 54.6 us -> 0 us
  Pallas kernels: 0 us -> 42.5 us
  waiting for transfers between devices: 146 us -> 114 us
  starting transfers between devices: 30.6 us -> 39.6 us
    all_to_all x3, waiting for transfers between devices: 117 us -> 11.8 us  [the longest x1 7.66 us: shards(): lax.all_to_all(outgoing, DP, split_axis=0, concat_axis=0, tiled=True)]
    dot_general x2 -> x0, matrix products: 54.6 us -> none  [the longest x1 44.4 us: contract_last(): lax.dot_general(left, right, (((1,), (1,)), ((), ())), preferred_element_...]
    reduce_scatter x0 -> x1, waiting for transfers between devices: none -> 45.2 us  [shards(): summed = lax.psum_scatter(partial, 'z', scatter_dimension=0, tiled=True)[0]]
    pallas_call x0 -> x6, Pallas kernels: none -> 42.5 us  [the longest x1 10.1 us: hidden_grad(): pl.pallas_call(hidden_grad_body, grid=(steps,), in_specs=[pl.BlockSpec((d...]
    unnamed x20, local copies, waits for them, and re-layouts: 44.1 us -> 2.41 us
    ppermute x0 -> x12, waiting for transfers between devices: none -> 38.5 us  [the longest x8 19.5 us: swap(): return lax.ppermute(value, axis, SWAP)]
    psum x1 -> x0, blocking collectives: 32.9 us -> none  [shards(): grad_step = scale_factor * lax.psum(partial_step, 'dp')]
    unnamed x1 -> x0, blocking collectives: 32.8 us -> none
  transfers between devices with their start and end apart: 6 -> 17, of which waited for: 5 -> 12; matrix products, arithmetic and copies ran while one was open for 33% -> 6% of each run, Pallas kernels for 0% -> 11%
where the time goes in v2:
time: 228 us
  waiting for transfers between devices  114 us (50%)
  Pallas kernels  42.5 us (19%)
  starting transfers between devices  39.6 us (17%)
  between operations  14.2 us (6%)
  other arithmetic  11.6 us (5%)
  local copies, waits for them, and re-layouts  6.22 us (3%)
    reduce_scatter x1, waiting for transfers between devices, shards(): summed = lax.psum_scatter(partial, 'z', scatter_dimension=0, tiled=True)[0]  45.2 us
    ppermute x8, waiting for transfers between devices, swap(): return lax.ppermute(value, axis, SWAP)  19.5 us
    ppermute x4, waiting for transfers between devices, shift(): lax.ppermute(value, axis, [(i, (i + by) % count) for i in range(count)])  19 us
    all_gather x1, waiting for transfers between devices, shards(): weight = lax.all_gather(weight, 'z', axis=0)  18.2 us
    all_to_all x1, starting transfers between devices, shards(): lax.all_to_all(picked, DP, split_axis=0, concat_axis=0, tiled=True)  10.5 us
    pallas_call x1, Pallas kernels, hidden_grad(): pl.pallas_call(hidden_grad_body, grid=(steps,), in_specs=[pl.BlockSpec((d...  10.1 us
    pallas_call x1, Pallas kernels, weight_grad(): pl.pallas_call(weight_grad_body, grid=(steps,), in_specs=[pl.BlockSpec((r...  9.65 us
    pallas_call x1, Pallas kernels, unpack(): pl.pallas_call(unpack_body, grid=(steps,), in_specs=[pl.BlockSpec((slots...  9.26 us
  transfers between devices with their start and end apart: 17, of which 12 were waited for; matrix products, arithmetic and copies ran while one was open for 6% of the time, Pallas kernels for 11%

profile of v2, /device:TPU:1, one launch (start us, length us, event | category | flops | bytes accessed | tf_op | source)
XLA Modules:
  0.0 227.8 jit_solution(16386520630522855026)
XLA Ops:
  7.2 3.8 %collective-permute-start = (bf16[64,3072]{1,0:T(8,128)(2,1)}, bf16[64,3072]{1,0:T(8,128)(2,1)S(1)}, u32[]{:S(2)}, u32[]{:S(2)}) collective-permute-start(bf16[64,3072]{1,0:T(8,128)(2,1)} %param.9), channel_id=1, source_target_pairs={{0,2},{2,0},{1,3},{3,1},{4,6},{6,4},{5,7},{7,5},{8,10},{10,8},{9,1... | collective-permute-start | bytes 1179656 | tf_op jit(solution)/shard_map/ppermute | solution.py:43
  11.7 3.2 %fusion.2 = bf16[192,768]{1,0:T(8,128)(2,1)S(1)} fusion(bf16[768,192]{0,1:T(8,128)(2,1)} %param.10, f32[192]{0:T(256)S(1)} %bitcast.63), kind=kLoop, calls=%fused_computation.11 | loop fusion | flops 1327104 | bytes 590592 | tf_op jit(solution)/shard_map/convert_element_type | solution.py:300
  15.4 1.0 constant_dynamic-update-slice_fusion.1
  16.5 2.7 %collective-permute-done = bf16[64,3072]{1,0:T(8,128)(2,1)S(1)} collective-permute-done((bf16[64,3072]{1,0:T(8,128)(2,1)}, bf16[64,3072]{1,0:T(8,128)(2,1)S(1)}, u32[]{:S(2)}, u32[]{:S(2)}) %collective-permute-start) | collective-permute-done | bytes 393248 | tf_op jit(solution)/shard_map/ppermute | solution.py:43
  19.2 7.3 %collective-permute-done.5 = bf16[192,768]{1,0:T(8,128)(2,1)S(1)} collective-permute-done((bf16[192,768]{1,0:T(8,128)(2,1)S(1)}, bf16[192,768]{1,0:T(8,128)(2,1)S(1)}, u32[]{:S(2)}, u32[]{:S(2)}) %collective-permute-start.5) | collective-permute-done | bytes 294944 | tf_op jit(solution)/shard_map/ppermute | solution.py:43
  27.4 1.3 collective-permute-start.1
  28.7 1.5 collective-permute-start.3
  30.2 16.1 %collective-permute-done.1.refs_2_ = bf16[128,3072]{1,0:T(8,128)(2,1)S(1)} collective-permute-done((bf16[128,3072]{1,0:T(8,128)(2,1)S(1)}, bf16[128,3072]{1,0:T(8,128)(2,1)S(1)}, u32[]{:S(2)}, u32[]{:S(2)}) %collective-permute-start.1) | collective-permute-done | bytes 786464 | tf_op jit(solution)/shard_map/ppermute | solution.py:48
  46.5 2.7 %collective-permute-start.4 = (bf16[64,3072]{1,0:T(8,128)(2,1)S(1)}, bf16[64,3072]{1,0:T(8,128)(2,1)S(1)}, u32[]{:S(2)}, u32[]{:S(2)}) collective-permute-start(bf16[64,3072]{1,0:T(8,128)(2,1)S(1)} %slice.37), channel_id=1, source_target_pairs={{0,12},{4,0},{8,4},{12,8},{1,13},{5,1},{9,5},{13,9},{2,14},{6,2},{... | collective-permute-start | bytes 1179656 | tf_op jit(solution)/shard_map/ppermute | solution.py:48
  49.8 3.3 %split_columns.1 = bf16[16,136,768]{2,1,0:T(8,128)(2,1)} custom-call(bf16[128,12288]{1,0:T(8,128)(2,1)} %source.1, bf16[8,768]{1,0:T(8,128)(2,1)} %fusion.8.codes), custom_call_target="tpu_custom_call" | custom-call | bytes 6291456 | tf_op jit(solution)/shard_map/split_columns/pallas_call | solution.py:62
  53.1 2.8 %collective-permute-done.2.refs_6_ = bf16[64,3072]{1,0:T(8,128)(2,1)S(1)} collective-permute-done((bf16[64,3072]{1,0:T(8,128)(2,1)S(1)}, bf16[64,3072]{1,0:T(8,128)(2,1)S(1)}, u32[]{:S(2)}, u32[]{:S(2)}) %collective-permute-start.2) | collective-permute-done | bytes 393248 | tf_op jit(solution)/shard_map/ppermute | solution.py:48
  56.9 8.6 %all-to-all-start = ((bf16[16,136,768]{2,1,0:T(8,128)(2,1)}), bf16[16,136,768]{2,1,0:T(8,128)(2,1)S(1)}, u32[]{:S(2)}, u32[]{:S(2)}) async-start(bf16[16,136,768]{2,1,0:T(8,128)(2,1)} %split_columns.1), calls=%async_computation | async-start | bytes 6684672 | tf_op jit(solution)/shard_map/all_to_all | solution.py:330
  66.7 1.5 collective-permute-done.6.refs_1_
  68.2 2.8 %collective-permute-done.9.refs_8_ = bf16[64,3072]{1,0:T(8,128)(2,1)} collective-permute-done((bf16[64,3072]{1,0:T(8,128)(2,1)}, bf16[64,3072]{1,0:T(8,128)(2,1)}, u32[]{:S(2)}, u32[]{:S(2)}) %collective-permute-start.9) | collective-permute-done | bytes 393248 | tf_op jit(solution)/shard_map/ppermute | solution.py:43
  71.6 18.2 %all-gather.3.cloned.1.call-done = bf16[16,192,768]{2,1,0:T(8,128)(2,1)} async-done(((bf16[2,192,768]{2,1,0:T(8,128)(2,1)}), bf16[16,192,768]{2,1,0:T(8,128)(2,1)}) %all-gather.3.cloned.1.call-update) | async-done | bytes 4718608 | tf_op jit(solution)/shard_map/all_gather | solution.py:325
  89.8 10.1 %hidden_grad.1.grad = f32[1024,768]{1,0:T(8,128)} custom-call(bf16[8,2,192,768]{3,2,1,0:T(8,128)(2,1)} %bitcast.66, bf16[128,3072]{1,0:T(8,128)(2,1)} %copy-done.5, bf16[128,3072]{1,0:T(8,128)(2,1)} %collective-permute-done.6.refs_1_, bf16[128,3072]{1,0:T(8,128)(2,1)} %copy-done.3, bf16[128,3072]{1,0:T(8,128)(2,1)} %collective-permute-done.7.refs_3_, ...), custom_call_target="tpu_custom_call" | custom-call | flops 4831838208 | bytes 14155776 | tf_op jit(solution)/shard_map/hidden_grad/pallas_call | solution.py:204
  99.9 7.7 %all-to-all-done.incoming = bf16[16,136,768]{2,1,0:T(8,128)(2,1)S(1)} async-done(((bf16[16,136,768]{2,1,0:T(8,128)(2,1)}), bf16[16,136,768]{2,1,0:T(8,128)(2,1)S(1)}, u32[]{:S(2)}, u32[]{:S(2)}) %all-to-all-start) | async-done | bytes 3342368 | tf_op jit(solution)/shard_map/all_to_all | solution.py:330
  107.7 1.1 compare_select_fusion.8.place
  109.3 7.0 %pack.1 = (bf16[1024,768]{1,0:T(8,128)(2,1)}, bf16[1024,768]{1,0:T(8,128)(2,1)}) custom-call(s32[1,2048]{1,0:T(1,128)} %compare_select_fusion.8.place, bf16[16,136,768]{2,1,0:T(8,128)(2,1)} %copy-done.1), custom_call_target="tpu_custom_call" | custom-call | flops 3221225472 | bytes 6291456 | tf_op jit(solution)/shard_map/pack/pallas_call | solution.py:125
  116.2 9.6 %weight_grad.1 = bf16[8,2,192,768]{3,2,1,0:T(8,128)(2,1)} custom-call(bf16[1024,768]{1,0:T(8,128)(2,1)} %get-tuple-element.30.act, bf16[128,3072]{1,0:T(8,128)(2,1)} %copy-done.5, bf16[128,3072]{1,0:T(8,128)(2,1)} %collective-permute-done.6.refs_1_, bf16[128,3072]{1,0:T(8,128)(2,1)} %copy-done.3, bf16[128,3072]{1,0:T(8,128)(2,1)} %collective-permute-done.7.refs_3_, ...), custom_call_target="tpu_custom_call" | custom-call | flops 4831838208 | bytes 12582912 | tf_op jit(solution)/shard_map/weight_grad/pallas_call | solution.py:161
  125.9 1.4 copy.11.place
  127.3 9.3 %unpack.1 = bf16[16,128,768]{2,1,0:T(8,128)(2,1)} custom-call(s32[2048,1]{1,0:T(8,128)} %copy.11.place, bf16[1024,768]{1,0:T(8,128)(2,1)} %get-tuple-element.33.packed, f32[1024,768]{1,0:T(8,128)} %hidden_grad.1.grad), custom_call_target="tpu_custom_call" | custom-call | flops 3221225472 | bytes 7864320 | tf_op jit(solution)/shard_map/unpack/pallas_call | solution.py:243
  136.6 10.5 %all-to-all-start.1 = ((bf16[16,128,768]{2,1,0:T(8,128)(2,1)}), bf16[16,128,768]{2,1,0:T(8,128)(2,1)S(1)}, u32[]{:S(2)}, u32[]{:S(2)}) async-start(bf16[16,128,768]{2,1,0:T(8,128)(2,1)} %unpack.1), calls=%async_computation.1 | async-start | bytes 6291456 | tf_op jit(solution)/shard_map/all_to_all | solution.py:351
  147.1 45.2 %reduce-scatter.2.cloned.1.call-done = bf16[1,2,192,768]{3,2,1,0:T(8,128)(2,1)} async-done(((bf16[8,2,192,768]{3,2,1,0:T(8,128)(2,1)}), bf16[1,2,192,768]{3,2,1,0:T(8,128)(2,1)}) %reduce-scatter.2.cloned.1.call-update) | async-done | bytes 589840 | tf_op jit(solution)/shard_map/reduce_scatter | solution.py:345
  192.2 1.7 dynamic-slice_bitcast_fusion
  193.9 1.2 collective-permute-start.11
  195.1 2.4 %fusion.1 = (f32[192,768]{1,0:T(8,128)S(1)}, f32[192,768]{1,0:T(8,128)S(1)}) fusion(bf16[768,192]{0,1:T(8,128)(2,1)S(1)} %copy-done.2, f32[192]{0:T(256)S(1)} %bitcast.64), kind=kLoop, calls=%fused_computation.5 | loop fusion | flops 2064384 | bytes 1475328 | tf_op jit(solution)/shard_map/sub | solution.py:334
  197.5 4.6 %collective-permute-done.11 = bf16[192,768]{1,0:T(8,128)(2,1)} collective-permute-done((bf16[192,768]{1,0:T(8,128)(2,1)}, bf16[192,768]{1,0:T(8,128)(2,1)}, u32[]{:S(2)}, u32[]{:S(2)}) %collective-permute-start.11) | collective-permute-done | bytes 294944 | tf_op jit(solution)/shard_map/ppermute | solution.py:43
  202.2 2.0 multiply_reduce_fusion
  204.8 8.2 %all-to-all-start.2 = ((f32[16,1,192]{2,1,0:T(1,128)}), f32[16,1,192]{2,1,0:T(1,128)S(1)}, u32[]{:S(2)}, u32[]{:S(2)}) async-start(f32[16,1,192]{2,1,0:T(1,128)} %broadcast_in_dim.19), calls=%async_computation.3 | async-start | bytes 32768 | tf_op jit(solution)/shard_map/all_to_all | solution.py:356
  213.0 3.2 %join_columns.1 = bf16[128,12288]{1,0:T(8,128)(2,1)} custom-call(bf16[16,128,768]{2,1,0:T(8,128)(2,1)} %copy-done), custom_call_target="tpu_custom_call" | custom-call | bytes 6291456 | tf_op jit(solution)/shard_map/join_columns/pallas_call | solution.py:86
  216.2 4.1 %all-to-all-done.2 = f32[16,1,192]{2,1,0:T(1,128)S(1)} async-done(((f32[16,1,192]{2,1,0:T(1,128)}), f32[16,1,192]{2,1,0:T(1,128)S(1)}, u32[]{:S(2)}, u32[]{:S(2)}) %all-to-all-start.2) | async-done | bytes 12320 | tf_op jit(solution)/shard_map/all_to_all | solution.py:356
  (49 shorter events, 7.5 us)
Async XLA Ops:
  7.2 82.6 %all-gather.3.cloned.1.call-start = ((), (), s32[]{:S(2)}) async-start(), calls=%async_computation.5 | async-start | bytes 5308416 | tf_op jit(solution)/shard_map/all_gather | solution.py:325
  7.2 11.9 %collective-permute-start = (bf16[64,3072]{1,0:T(8,128)(2,1)}, bf16[64,3072]{1,0:T(8,128)(2,1)S(1)}, u32[]{:S(2)}, u32[]{:S(2)}) collective-permute-start(bf16[64,3072]{1,0:T(8,128)(2,1)} %param.9), channel_id=1, source_target_pairs={{0,2},{2,0},{1,3},{3,1},{4,6},{6,4},{5,7},{7,5},{8,10},{10,8},{9,1... | collective-permute-start | bytes 1179656 | tf_op jit(solution)/shard_map/ppermute | solution.py:43
  14.9 34.3 %copy-start.8 = (s32[128]{0:T(128)S(1)}, s32[128]{0:T(128)}, u32[]{:S(2)}) copy-start(s32[128]{0:T(128)} %param.8) | copy-start | bytes 1540
  15.0 11.5 %collective-permute-start.5 = (bf16[192,768]{1,0:T(8,128)(2,1)S(1)}, bf16[192,768]{1,0:T(8,128)(2,1)S(1)}, u32[]{:S(2)}, u32[]{:S(2)}) collective-permute-start(bf16[192,768]{1,0:T(8,128)(2,1)S(1)} %fusion.2), channel_id=1, source_target_pairs={{0,128},{128,0},{1,129},{129,1},{2,130},{130,2},{3,131},{131,3},{4... | collective-permute-start | bytes 884744 | tf_op jit(solution)/shard_map/ppermute | solution.py:43
  19.2 34.0 %copy-start.5 = (bf16[128,3072]{1,0:T(8,128)(2,1)}, bf16[128,3072]{1,0:T(8,128)(2,1)S(1)}, u32[]{:S(2)}) copy-start(bf16[128,3072]{1,0:T(8,128)(2,1)S(1)} %constant_dynamic-update-slice_fusion.refs_0_) | copy-start | bytes 2359300
  27.4 18.9 %collective-permute-start.1 = (bf16[128,3072]{1,0:T(8,128)(2,1)S(1)}, bf16[128,3072]{1,0:T(8,128)(2,1)S(1)}, u32[]{:S(2)}, u32[]{:S(2)}) collective-permute-start(bf16[128,3072]{1,0:T(8,128)(2,1)S(1)} %constant_dynamic-update-slice_fusion.refs_0_), channel_id=1, source_target_pairs={{0,4},{4,8},{8,12},{12,0},{1,5},{5,9},{9,13},{13,1},{2,6},{6,10},{... | collective-permute-start | bytes 2359304 | tf_op jit(solution)/shard_map/ppermute | solution.py:48
  28.7 17.7 %collective-permute-start.3 = (bf16[128,3072]{1,0:T(8,128)(2,1)S(1)}, bf16[128,3072]{1,0:T(8,128)(2,1)S(1)}, u32[]{:S(2)}, u32[]{:S(2)}) collective-permute-start(bf16[128,3072]{1,0:T(8,128)(2,1)S(1)} %constant_dynamic-update-slice_fusion.refs_0_), channel_id=1, source_target_pairs={{0,12},{4,0},{8,4},{12,8},{1,13},{5,1},{9,5},{13,9},{2,14},{6,2},{... | collective-permute-start | bytes 2359304 | tf_op jit(solution)/shard_map/ppermute | solution.py:48
  46.3 2.9 %copy-start.3 = (bf16[128,3072]{1,0:T(8,128)(2,1)}, bf16[128,3072]{1,0:T(8,128)(2,1)S(1)}, u32[]{:S(2)}) copy-start(bf16[128,3072]{1,0:T(8,128)(2,1)S(1)} %collective-permute-done.1.refs_2_) | copy-start | bytes 2359300
  46.3 9.6 %collective-permute-start.2 = (bf16[64,3072]{1,0:T(8,128)(2,1)S(1)}, bf16[64,3072]{1,0:T(8,128)(2,1)S(1)}, u32[]{:S(2)}, u32[]{:S(2)}) collective-permute-start(bf16[64,3072]{1,0:T(8,128)(2,1)S(1)} %slice.36), channel_id=1, source_target_pairs={{0,4},{4,8},{8,12},{12,0},{1,5},{5,9},{9,13},{13,1},{2,6},{6,10},{... | collective-permute-start | bytes 1179656 | tf_op jit(solution)/shard_map/ppermute | solution.py:48
  46.4 2.8 %copy-start.4 = (bf16[128,3072]{1,0:T(8,128)(2,1)}, bf16[128,3072]{1,0:T(8,128)(2,1)S(1)}, u32[]{:S(2)}) copy-start(bf16[128,3072]{1,0:T(8,128)(2,1)S(1)} %collective-permute-done.3.refs_4_) | copy-start | bytes 2359300
  46.5 9.5 %collective-permute-start.4 = (bf16[64,3072]{1,0:T(8,128)(2,1)S(1)}, bf16[64,3072]{1,0:T(8,128)(2,1)S(1)}, u32[]{:S(2)}, u32[]{:S(2)}) collective-permute-start(bf16[64,3072]{1,0:T(8,128)(2,1)S(1)} %slice.37), channel_id=1, source_target_pairs={{0,12},{4,0},{8,4},{12,8},{1,13},{5,1},{9,5},{13,9},{2,14},{6,2},{... | collective-permute-start | bytes 1179656 | tf_op jit(solution)/shard_map/ppermute | solution.py:48
  56.0 0.8 copy-start.6
  56.0 0.9 copy-start.7
  56.9 50.7 %all-to-all-start = ((bf16[16,136,768]{2,1,0:T(8,128)(2,1)}), bf16[16,136,768]{2,1,0:T(8,128)(2,1)S(1)}, u32[]{:S(2)}, u32[]{:S(2)}) async-start(bf16[16,136,768]{2,1,0:T(8,128)(2,1)} %split_columns.1), calls=%async_computation | async-start | bytes 6684672 | tf_op jit(solution)/shard_map/all_to_all | solution.py:330
  65.4 126.8 %reduce-scatter.2.cloned.1.call-start = ((), (), s32[]{:S(2)}) async-start(), calls=%async_computation.4 | async-start | bytes 5308416 | tf_op jit(solution)/shard_map/reduce_scatter | solution.py:345
  65.5 2.7 %collective-permute-start.6 = (bf16[128,3072]{1,0:T(8,128)(2,1)}, bf16[128,3072]{1,0:T(8,128)(2,1)}, u32[]{:S(2)}, u32[]{:S(2)}) collective-permute-start(bf16[128,3072]{1,0:T(8,128)(2,1)} %copy-done.5), channel_id=1, source_target_pairs={{0,1},{1,0},{2,3},{3,2},{4,5},{5,4},{6,7},{7,6},{8,9},{9,8},{10,11... | collective-permute-start | bytes 2359304 | tf_op jit(solution)/shard_map/ppermute | solution.py:43
  65.7 5.9 %collective-permute-start.7 = (bf16[128,3072]{1,0:T(8,128)(2,1)}, bf16[128,3072]{1,0:T(8,128)(2,1)}, u32[]{:S(2)}, u32[]{:S(2)}) collective-permute-start(bf16[128,3072]{1,0:T(8,128)(2,1)} %copy-done.3), channel_id=1, source_target_pairs={{0,1},{1,0},{2,3},{3,2},{4,5},{5,4},{6,7},{7,6},{8,9},{9,8},{10,11... | collective-permute-start | bytes 2359304 | tf_op jit(solution)/shard_map/ppermute | solution.py:43
  66.1 5.5 %collective-permute-start.8 = (bf16[128,3072]{1,0:T(8,128)(2,1)}, bf16[128,3072]{1,0:T(8,128)(2,1)}, u32[]{:S(2)}, u32[]{:S(2)}) collective-permute-start(bf16[128,3072]{1,0:T(8,128)(2,1)} %copy-done.4), channel_id=1, source_target_pairs={{0,1},{1,0},{2,3},{3,2},{4,5},{5,4},{6,7},{7,6},{8,9},{9,8},{10,11... | collective-permute-start | bytes 2359304 | tf_op jit(solution)/shard_map/ppermute | solution.py:43
  66.2 4.8 %collective-permute-start.9 = (bf16[64,3072]{1,0:T(8,128)(2,1)}, bf16[64,3072]{1,0:T(8,128)(2,1)}, u32[]{:S(2)}, u32[]{:S(2)}) collective-permute-start(bf16[64,3072]{1,0:T(8,128)(2,1)} %copy-done.6), channel_id=1, source_target_pairs={{0,1},{1,0},{2,3},{3,2},{4,5},{5,4},{6,7},{7,6},{8,9},{9,8},{10,11... | collective-permute-start | bytes 1179656 | tf_op jit(solution)/shard_map/ppermute | solution.py:43
  66.6 5.0 %collective-permute-start.10 = (bf16[64,3072]{1,0:T(8,128)(2,1)}, bf16[64,3072]{1,0:T(8,128)(2,1)}, u32[]{:S(2)}, u32[]{:S(2)}) collective-permute-start(bf16[64,3072]{1,0:T(8,128)(2,1)} %copy-done.7), channel_id=1, source_target_pairs={{0,1},{1,0},{2,3},{3,2},{4,5},{5,4},{6,7},{7,6},{8,9},{9,8},{10,11... | collective-permute-start | bytes 1179656 | tf_op jit(solution)/shard_map/ppermute | solution.py:43
  107.6 1.7 copy-start.1
  136.6 58.5 %copy-start.2 = (bf16[768,192]{0,1:T(8,128)(2,1)S(1)}, bf16[768,192]{0,1:T(8,128)(2,1)}, u32[]{:S(2)}) copy-start(bf16[768,192]{0,1:T(8,128)(2,1)} %param.10) | copy-start | bytes 884740
  136.6 67.6 %all-to-all-start.1 = ((bf16[16,128,768]{2,1,0:T(8,128)(2,1)}), bf16[16,128,768]{2,1,0:T(8,128)(2,1)S(1)}, u32[]{:S(2)}, u32[]{:S(2)}) async-start(bf16[16,128,768]{2,1,0:T(8,128)(2,1)} %unpack.1), calls=%async_computation.1 | async-start | bytes 6291456 | tf_op jit(solution)/shard_map/all_to_all | solution.py:351
  193.9 8.3 %collective-permute-start.11 = (bf16[192,768]{1,0:T(8,128)(2,1)}, bf16[192,768]{1,0:T(8,128)(2,1)}, u32[]{:S(2)}, u32[]{:S(2)}) collective-permute-start(bf16[192,768]{1,0:T(8,128)(2,1)} %dynamic-slice_bitcast_fusion), channel_id=1, source_target_pairs={{0,128},{128,0},{1,129},{129,1},{2,130},{130,2},{3,131},{131,3},{4... | collective-permute-start | bytes 884744 | tf_op jit(solution)/shard_map/ppermute | solution.py:43
  204.2 8.8 %copy-start = (bf16[16,128,768]{2,1,0:T(8,128)(2,1)}, bf16[16,128,768]{2,1,0:T(8,128)(2,1)S(1)}, u32[]{:S(2)}) copy-start(bf16[16,128,768]{2,1,0:T(8,128)(2,1)S(1)} %all-to-all-done.1.source) | copy-start | bytes 9437188
  204.8 15.5 %all-to-all-start.2 = ((f32[16,1,192]{2,1,0:T(1,128)}), f32[16,1,192]{2,1,0:T(1,128)S(1)}, u32[]{:S(2)}, u32[]{:S(2)}) async-start(f32[16,1,192]{2,1,0:T(1,128)} %broadcast_in_dim.19), calls=%async_computation.3 | async-start | bytes 32768 | tf_op jit(solution)/shard_map/all_to_all | solution.py:356
Sparse Core Ops, SparseCore 0:
  27.5 62.2 all-gather.2
  126.0 66.1 reduce-scatter.1

commit v3 on v2

v3 whole, which is shorter than its diff:
```python
import functools

import jax
import jax.numpy as jnp
from jax import lax
from jax.experimental import pallas as pl
from jax.experimental.pallas import tpu as pltpu
from jax.sharding import Mesh, PartitionSpec as P

FF_W = 12288

top_level = 7.0
wobble = 0.9
two_pi = 6.283185307179586
inv_root_two = 0.7071067811865476
inv_root_tau = 0.3989422804014327

PARTS = ("a", "z", "x", "b", "c")
SIZES = (2, 8, 4, 2, 2)
FSDP = ("a", "z")
DP = ("x", "b", "c")
SWAP = [(0, 1), (1, 0)]

ON_CHIP = pl.BlockSpec(memory_space=pltpu.VMEM)
LARGE_VMEM = pltpu.CompilerParams(vmem_limit_bytes=50 * 1024 * 1024)
SMALL_VMEM = pltpu.CompilerParams(vmem_limit_bytes=24 * 1024 * 1024)


def gelu_pair(values):
    normal_cdf = 0.5 * (1.0 + lax.erf(values * inv_root_two))
    density = jnp.exp(-0.5 * values * values) * inv_root_tau
    return (values * normal_cdf, normal_cdf + values * density)


def soft_quantize(weight, step):
    ratio = weight / step
    clipped = top_level * jnp.tanh(ratio / top_level)
    phase = two_pi * clipped
    quantized = clipped - wobble * jnp.sin(phase) / two_pi
    slope = (1.0 - wobble * jnp.cos(phase)) * (1.0 - clipped / top_level * (clipped / top_level))
    return (quantized, slope, ratio)


def swap(value, axis):
    return lax.ppermute(value, axis, SWAP)


def shift(value, axis, by):
    count = lax.axis_size(axis)
    return lax.ppermute(value, axis, [(i, (i + by) % count) for i in range(count)])


def split_columns_body(width, source, codes, target):
    rows = source.shape[0]
    for k in range(target.shape[0]):
        target[k, :rows] = source[:, k * width : (k + 1) * width]
        target[k, rows:] = codes[...]


def split_columns(values, codes, count):
    rows, width = values.shape[0], values.shape[1] // count
    many = count // 2
    tall = rows + codes.shape[0]
    return pl.pallas_call(
        functools.partial(split_columns_body, width),
        grid=(count // many,),
        in_specs=[
            pl.BlockSpec((rows, many * width), lambda i: (0, i)),
            pl.BlockSpec(codes.shape, lambda i: (0, 0)),
        ],
        out_specs=pl.BlockSpec((many, tall, width), lambda i: (i, 0, 0)),
        out_shape=jax.ShapeDtypeStruct((count, tall, width), values.dtype),
        cost_estimate=pl.CostEstimate(
            flops=0, bytes_accessed=4 * values.size, transcendentals=0
        ),
        name="split_columns",
    )(values, codes)


def join_columns_body(width, source, target):
    many = target.shape[1] // width
    first = pl.program_id(0) * many
    for k in range(many):
        target[:, k * width : (k + 1) * width] = source[first + k]


def join_columns(values):
    count, rows, width = values.shape
    many = count // 2
    return pl.pallas_call(
        functools.partial(join_columns_body, width),
        grid=(count // many,),
        in_specs=[ON_CHIP],
        out_specs=pl.BlockSpec((rows, many * width), lambda i: (0, i)),
        out_shape=jax.ShapeDtypeStruct((rows, count * width), values.dtype),
        compiler_params=SMALL_VMEM,
        cost_estimate=pl.CostEstimate(
            flops=0, bytes_accessed=4 * values.size, transcendentals=0
        ),
        name="join_columns",
    )(values)


def contract_rows(left, right):
    return lax.dot_general(
        left, right, (((0,), (0,)), ((), ())), preferred_element_type=jnp.float32
    )


def pack_body(place, incoming, packed, act):
    part, hidden = 256, packed.shape[1]
    slots = place.shape[1]
    each = slots // incoming.shape[0]
    start = pl.multiple_of(pl.program_id(0) * part, part)
    row = start + lax.broadcasted_iota(jnp.int32, (part, slots), 0)
    pick = jnp.where(row == place[...], 1.0, 0.0).astype(jnp.bfloat16)
    source = incoming[:, :each, :].reshape(slots, hidden)
    found = jnp.dot(pick, source, preferred_element_type=jnp.float32)
    packed[pl.ds(start, part), :] = narrow(found)
    act[pl.ds(start, part), :] = narrow(gelu_pair(found)[0])


def pack(place, incoming, rows):
    hidden = incoming.shape[2]
    slots = place.shape[1]
    return pl.pallas_call(
        pack_body,
        grid=(rows // 256,),
        in_specs=[pl.BlockSpec((1, slots), lambda i: (0, 0)), ON_CHIP],
        out_specs=[ON_CHIP, ON_CHIP],
        out_shape=[jax.ShapeDtypeStruct((rows, hidden), jnp.bfloat16)] * 2,
        compiler_params=SMALL_VMEM,
        cost_estimate=pl.CostEstimate(
            flops=2 * rows * hidden * slots,
            bytes_accessed=2 * slots * hidden + 4 * rows * hidden,
            transcendentals=rows * hidden,
        ),
        name="pack",
    )(place, incoming)


def stacked(pieces):
    return jnp.concatenate([piece[...] for piece in pieces])


def weight_grad_body(act, *refs):
    pieces, out = refs[:-1], refs[-1]
    grad = contract_rows(stacked(pieces), act[...])
    out[...] = narrow(grad).reshape(out.shape)


def weight_grad(act, pieces, count, sides, width):
    rows, hidden = act.shape
    outputs = pieces[0].shape[1]
    steps = 4
    deep = outputs // steps // width
    around = count // deep
    return pl.pallas_call(
        weight_grad_body,
        grid=(steps,),
        in_specs=[ON_CHIP]
        + [pl.BlockSpec((piece.shape[0], outputs // steps), lambda i: (0, i)) for piece in pieces],
        out_specs=pl.BlockSpec(
            (deep, 1, width, hidden), lambda i: (i % around, i // around, 0, 0)
        ),
        out_shape=jax.ShapeDtypeStruct((count, sides, width, hidden), jnp.bfloat16),
        compiler_params=LARGE_VMEM,
        cost_estimate=pl.CostEstimate(
            flops=2 * rows * hidden * outputs,
            bytes_accessed=2 * rows * (outputs + hidden) + 2 * outputs * hidden,
            transcendentals=0,
        ),
        name="weight_grad",
    )(act, *pieces)


def near_grad_body(weight, *refs):
    pieces, total = refs[:-1], refs[-1]
    step = pl.program_id(0)
    tile = weight.shape[0] * weight.shape[2]
    grads = stacked(pieces)
    block = weight[...].reshape(tile, total.shape[1])
    grad = jnp.dot(grads, block, preferred_element_type=jnp.float32)

    @pl.when(step == 0)
    def _():
        total[...] = grad

    @pl.when(step > 0)
    def _():
        total[...] += grad


def hidden_specs(pieces, weight, steps):
    tile = pieces[0].shape[1] // steps
    count, sides, width, hidden = weight.shape
    deep = tile // width
    around = count // deep
    return [
        pl.BlockSpec((deep, 1, width, hidden), lambda i: (i % around, i // around, 0, 0)),
    ] + [pl.BlockSpec((piece.shape[0], tile), lambda i: (0, i)) for piece in pieces]


def hidden_cost(rows, weight, transcendentals):
    hidden = weight.shape[-1]
    outputs = weight.size // hidden
    return pl.CostEstimate(
        flops=2 * rows * hidden * outputs,
        bytes_accessed=2 * rows * outputs + 2 * outputs * hidden + 4 * rows * hidden,
        transcendentals=transcendentals,
    )


def near_grad(pieces, weight):
    rows = sum(piece.shape[0] for piece in pieces)
    hidden = weight.shape[-1]
    steps = 4
    return pl.pallas_call(
        near_grad_body,
        grid=(steps,),
        in_specs=hidden_specs(pieces, weight, steps),
        out_specs=ON_CHIP,
        out_shape=jax.ShapeDtypeStruct((rows, hidden), jnp.float32),
        compiler_params=LARGE_VMEM,
        cost_estimate=hidden_cost(rows, weight, 0),
        name="near_grad",
    )(weight, *pieces)


def hidden_grad_body(steps, packed, near, weight, *refs):
    pieces, (out, total) = refs[:-2], refs[-2:]
    step = pl.program_id(0)
    rows = near.shape[0]

    def slope(some):
        return gelu_pair(wide(packed[some, :]))[1]

    part = rows // steps
    some = pl.ds(pl.multiple_of(step * part, part), part)
    out[some, :] = narrow(near[some, :] * slope(some))

    tile = weight.shape[0] * weight.shape[2]
    grads = stacked(pieces)
    block = weight[...].reshape(tile, total.shape[1])
    grad = jnp.dot(grads, block, preferred_element_type=jnp.float32)

    @pl.when(step == 0)
    def _():
        total[...] = grad

    @pl.when((step > 0) & (step < steps - 1))
    def _():
        total[...] += grad

    @pl.when(step == steps - 1)
    def _():
        rest = pl.ds(rows, total.shape[0])
        out[rest, :] = narrow((total[...] + grad) * slope(rest))


def hidden_grad(packed, near, pieces, weight):
    rows = sum(piece.shape[0] for piece in pieces)
    total, hidden = near.shape[0] + rows, weight.shape[-1]
    steps = 4
    return pl.pallas_call(
        functools.partial(hidden_grad_body, steps),
        grid=(steps,),
        in_specs=[ON_CHIP, ON_CHIP] + hidden_specs(pieces, weight, steps),
        out_specs=ON_CHIP,
        out_shape=jax.ShapeDtypeStruct((total, hidden), jnp.bfloat16),
        scratch_shapes=[pltpu.VMEM((rows, hidden), jnp.float32)],
        compiler_params=LARGE_VMEM,
        cost_estimate=hidden_cost(rows, weight, total * hidden),
        name="hidden_grad",
    )(packed, near, weight, *pieces)


def unpack_body(place, grad, out):
    slots, rows = place.shape[0], grad.shape[0]
    column = lax.broadcasted_iota(jnp.int32, (slots, rows), 1)
    pick = jnp.where(column == place[...], 1.0, 0.0).astype(jnp.bfloat16)
    found = jnp.dot(pick, grad[...], preferred_element_type=jnp.float32)
    out[...] = narrow(found).reshape(out.shape)


def unpack(place, grad, owners):
    rows, hidden = grad.shape
    slots = place.shape[0]
    steps = 4
    return pl.pallas_call(
        unpack_body,
        grid=(steps,),
        in_specs=[
            pl.BlockSpec((slots // steps, 1), lambda i: (i, 0)),
            ON_CHIP,
        ],
        out_specs=pl.BlockSpec(
            (owners // steps, slots // owners, hidden), lambda i: (i, 0, 0)
        ),
        out_shape=jax.ShapeDtypeStruct((owners, slots // owners, hidden), jnp.bfloat16),
        compiler_params=SMALL_VMEM,
        cost_estimate=pl.CostEstimate(
            flops=2 * rows * hidden * slots,
            bytes_accessed=2 * slots * hidden + 2 * rows * hidden,
            transcendentals=0,
        ),
        name="unpack",
    )(place, grad)


def gather_near(own, first):
    half = own.shape[0]
    pair = after(jnp.concatenate([own, swap(own, "b")]), first)
    above, below = shift(pair, "x", 1), shift(pair, "x", -1)
    near = [pair, swap(pair, "c"), above, swap(above, "c"), below, swap(below, "c")]
    ends = lax.optimization_barrier((above[:half], below[half:]))
    return near, ends


def gather_far(ends, first):
    far_first, far_second = shift(ends[0], "x", 1), shift(ends[1], "x", -1)
    far_first, far_second, _ = lax.optimization_barrier((far_first, far_second, first))
    return [far_first, far_second, swap(far_first, "c"), swap(far_second, "c")]


def places(slots, block):
    x, b, c = (lax.axis_index(name) for name in DP)
    owner = slots // block
    away = (owner // 4 - x) % 4
    turn = jnp.where(away == 0, 0, jnp.where(away == 3, 1, away + 1))
    other_b = (owner // 2 + b) % 2
    other_c = (owner + c) % 2
    where = ((turn * 2 + other_c) * 2 + other_b) * block + slots % block
    return jnp.where(slots < 16 * block, where, 32 * block)


def narrow(value):
    return value.astype(jnp.bfloat16)


def wide(value):
    return value.astype(jnp.float32)


def after(value, *others):
    return lax.optimization_barrier((value, *others))[0]


def shards(patch_acts, patch_slot, out_grads, latent_weight, step_size):
    capacity, features = patch_acts.shape
    block = out_grads.shape[0]
    hidden, width = latent_weight.shape

    a = lax.axis_index("a")

    codes = jnp.concatenate([patch_slot // 32, patch_slot % 32]).astype(jnp.bfloat16)
    codes = jnp.zeros((8, hidden), jnp.bfloat16).at[0, : 2 * capacity].set(codes)
    outgoing = split_columns(patch_acts, codes, 16)
    near, ends = gather_near(out_grads, outgoing)

    step_column = wide(step_size).reshape(width, 1)
    latent = wide(latent_weight.T)
    weight = narrow(step_column * soft_quantize(latent, step_column)[0])
    weight = lax.optimization_barrier(weight)
    other = after(swap(weight, "a"), near[0])
    weight = jnp.stack([jnp.where(a == 0, weight, other), jnp.where(a == 0, other, weight)])
    weight = lax.all_gather(weight, "z", axis=0)

    latent = wide(after(latent_weight, near[0]).T)
    quantized, slope, ratio = soft_quantize(latent, step_column)
    slope, pull = lax.optimization_barrier((slope, quantized - ratio * slope))
    pull_other = swap(pull, "a")

    outgoing = after(outgoing, *ends, pull_other)
    incoming = lax.all_to_all(outgoing, DP, split_axis=0, concat_axis=0, tiled=True)
    near_part = near_grad(near, weight)
    incoming, near_part = lax.optimization_barrier((incoming, near_part))

    codes = incoming[:, capacity, : 2 * capacity].astype(jnp.int32)
    slots = codes[:, :capacity] * 32 + codes[:, capacity:]
    place = places(slots.reshape(16 * capacity), block)
    packed, act = pack(place.reshape(1, -1), incoming, 16 * block)
    far = gather_far(ends, act)
    column = after(place, act).reshape(-1, 1)
    partial = weight_grad(after(act, column), near + far, 8, 2, width)
    summed = lax.psum_scatter(partial, "z", scatter_dimension=0, tiled=True)[0]

    grad = hidden_grad(after(packed, partial), near_part, far, weight)
    picked = unpack(column, grad, 16)
    returned = lax.all_to_all(picked, DP, split_axis=0, concat_axis=0, tiled=True)
    grad_acts = join_columns(returned)

    mine = lax.dynamic_index_in_dim(summed, a, 0, False)
    other = lax.dynamic_index_in_dim(summed, 1 - a, 0, False)
    share = jnp.sum(wide(mine) * pull, axis=1)
    share_other = jnp.sum(wide(other) * pull_other, axis=1)
    shares = jnp.stack([jnp.where(a == 0, share, share_other), jnp.where(a == 0, share_other, share)])
    shares = jnp.broadcast_to(after(shares, returned)[:, None], (2, 16, width)).reshape(32, width)
    shares = lax.all_to_all(shares, ("a",) + DP, split_axis=0, concat_axis=0, tiled=True)

    grad_qweight = wide(mine) + wide(swap(other, "a"))
    grad_weight = (grad_qweight * slope).T
    shares = after(shares, grad_weight)
    scale_factor = (FF_W * top_level) ** (-0.5)
    grad_step = scale_factor * jnp.sum(shares, axis=0, keepdims=True)
    return (grad_acts, grad_weight, grad_step)


def solution(mesh):
    split = Mesh(mesh.devices.reshape(SIZES), PARTS)
    return jax.shard_map(
        shards,
        mesh=split,
        in_specs=(P(PARTS, None), P(PARTS), P(PARTS, None), P(DP, FSDP), P(None, FSDP)),
        out_specs=(P(PARTS, None), P(DP, FSDP), P(None, FSDP)),
        check_vma=False,
    )
```

time: 228 us -> 211 us (0.925)
  waiting for transfers between devices: 114 us -> 98.4 us
  Pallas kernels: 42.5 us -> 37.8 us
  starting transfers between devices: 39.6 us -> 35.3 us
  local copies, waits for them, and re-layouts: 6.22 us -> 10.5 us
  other arithmetic: 11.6 us -> 14.2 us
    all_gather x1, waiting for transfers between devices: 18.2 us -> 29.6 us  [shards(): weight = lax.all_gather(weight, 'z', axis=0)]
    ppermute x8 -> x9, waiting for transfers between devices: 19.5 us -> 9.85 us  [swap(): return lax.ppermute(value, axis, SWAP)]
    all_to_all x1, waiting for transfers between devices: 7.66 us -> 0.01 us  [shards(): lax.all_to_all(outgoing, DP, split_axis=0, concat_axis=0, tiled=True)]
    ppermute x4, waiting for transfers between devices: 19 us -> 11.7 us  [shift(): lax.ppermute(value, axis, [(i, (i + by) % count) for i in range(count)])]
    unnamed x20 -> x30, local copies, waits for them, and re-layouts: 2.41 us -> 7.79 us
    pallas_call x1, Pallas kernels: 9.26 us -> 4.51 us  [unpack(): pl.pallas_call(unpack_body, grid=(steps,), in_specs=[pl.BlockSpec((slots...]
    all_to_all x1, starting transfers between devices: 10.5 us -> 7.1 us  [shards(): lax.all_to_all(picked, DP, split_axis=0, concat_axis=0, tiled=True)]
    reduce_scatter x1, waiting for transfers between devices: 45.2 us -> 41.8 us  [shards(): summed = lax.psum_scatter(partial, 'z', scatter_dimension=0, tiled=True)[0]]
  transfers between devices with their start and end apart: 17 -> 18, of which waited for: 12 -> 9; matrix products, arithmetic and copies ran while one was open for 6% -> 6% of each run, Pallas kernels for 11% -> 14%
where the time goes in v3:
time: 211 us; the launch traced here: 210 us
  waiting for transfers between devices  98.4 us (47%)
  Pallas kernels  37.8 us (18%)
  starting transfers between devices  35.3 us (17%)
  other arithmetic  14.2 us (7%)
  between operations  14.2 us (7%)
  local copies, waits for them, and re-layouts  10.5 us (5%)
    reduce_scatter x1, waiting for transfers between devices, shards(): summed = lax.psum_scatter(partial, 'z', scatter_dimension=0, tiled=True)[0]  41.8 us
    all_gather x1, waiting for transfers between devices, shards(): weight = lax.all_gather(weight, 'z', axis=0)  29.6 us
    ppermute x4, waiting for transfers between devices, shift(): lax.ppermute(value, axis, [(i, (i + by) % count) for i in range(count)])  11.7 us
    ppermute x9, waiting for transfers between devices, swap(): return lax.ppermute(value, axis, SWAP)  9.85 us
    pallas_call x1, Pallas kernels, weight_grad(): pl.pallas_call(weight_grad_body, grid=(steps,), in_specs=[ON_CHIP] + [pl....  9.04 us
    ppermute x9, starting transfers between devices, swap(): return lax.ppermute(value, axis, SWAP)  8.14 us
    pallas_call x1, Pallas kernels, near_grad(): pl.pallas_call(near_grad_body, grid=(steps,), in_specs=hidden_specs(piece...  8.13 us
    unnamed x30, local copies, waits for them, and re-layouts  7.79 us
  transfers between devices with their start and end apart: 18, of which 9 were waited for; matrix products, arithmetic and copies ran while one was open for 6% of the time, Pallas kernels for 14%

profile of v3, /device:TPU:1, one launch (start us, length us, event | category | flops | bytes accessed | tf_op | source)
XLA Modules:
  0.0 210.3 jit_solution(11027756800966226927)
XLA Ops:
  7.2 3.8 %collective-permute-start = (bf16[64,3072]{1,0:T(8,128)(2,1)}, bf16[64,3072]{1,0:T(8,128)(2,1)S(1)}, u32[]{:S(2)}, u32[]{:S(2)}) collective-permute-start(bf16[64,3072]{1,0:T(8,128)(2,1)} %param.9), channel_id=1, source_target_pairs={{0,2},{2,0},{1,3},{3,1},{4,6},{6,4},{5,7},{7,5},{8,10},{10,8},{9,1... | collective-permute-start | bytes 1179656 | tf_op jit(solution)/shard_map/ppermute | solution.py:45
  11.7 3.2 %fusion.5 = bf16[192,768]{1,0:T(8,128)(2,1)S(1)} fusion(bf16[768,192]{0,1:T(8,128)(2,1)} %param.10, f32[192]{0:T(256)S(1)} %bitcast.72), kind=kLoop, calls=%fused_computation.15 | loop fusion | flops 1327104 | bytes 590592 | tf_op jit(solution)/shard_map/convert_element_type | solution.py:338
  16.7 3.3 %split_columns.1 = bf16[16,136,768]{2,1,0:T(8,128)(2,1)} custom-call(bf16[128,12288]{1,0:T(8,128)(2,1)} %source.1, bf16[8,768]{1,0:T(8,128)(2,1)} %fusion.11.codes), custom_call_target="tpu_custom_call" | custom-call | bytes 6291456 | tf_op jit(solution)/shard_map/split_columns/pallas_call | solution.py:64
  20.1 6.4 %collective-permute-done.4 = bf16[192,768]{1,0:T(8,128)(2,1)S(1)} collective-permute-done((bf16[192,768]{1,0:T(8,128)(2,1)S(1)}, bf16[192,768]{1,0:T(8,128)(2,1)S(1)}, u32[]{:S(2)}, u32[]{:S(2)}) %collective-permute-start.4) | collective-permute-done | bytes 294944 | tf_op jit(solution)/shard_map/ppermute | solution.py:45
  27.4 1.3 collective-permute-start.1
  28.7 1.5 collective-permute-start.2
  30.2 3.4 %fusion.4 = (f32[192,768]{1,0:T(8,128)S(1)}, f32[192,768]{1,0:T(8,128)}) fusion(bf16[768,192]{0,1:T(8,128)(2,1)S(1)} %copy-done.12, f32[192]{0:T(256)S(1)} %bitcast.73), kind=kLoop, calls=%fused_computation.10 | loop fusion | flops 2064384 | bytes 1475328 | tf_op jit(solution)/shard_map/sub | solution.py:371
  34.6 11.7 %collective-permute-done.1.refs_2_ = bf16[128,3072]{1,0:T(8,128)(2,1)S(1)} collective-permute-done((bf16[128,3072]{1,0:T(8,128)(2,1)S(1)}, bf16[128,3072]{1,0:T(8,128)(2,1)S(1)}, u32[]{:S(2)}, u32[]{:S(2)}) %collective-permute-start.1) | collective-permute-done | bytes 786464 | tf_op jit(solution)/shard_map/ppermute | solution.py:50
  48.3 6.9 %all-to-all-start = ((bf16[16,136,768]{2,1,0:T(8,128)(2,1)}), bf16[16,136,768]{2,1,0:T(8,128)(2,1)S(1)}, u32[]{:S(2)}, u32[]{:S(2)}) async-start(bf16[16,136,768]{2,1,0:T(8,128)(2,1)} %split_columns.1), calls=%async_computation | async-start | bytes 6684672 | tf_op jit(solution)/shard_map/all_to_all | solution.py:375
  56.0 1.6 collective-permute-start.8
  57.6 1.2 collective-permute-start.9
  60.2 29.6 %all-gather.3.cloned.1.call-done = bf16[16,192,768]{2,1,0:T(8,128)(2,1)} async-done(((bf16[2,192,768]{2,1,0:T(8,128)(2,1)}), bf16[16,192,768]{2,1,0:T(8,128)(2,1)}) %all-gather.3.cloned.1.call-update) | async-done | bytes 4718608 | tf_op jit(solution)/shard_map/all_gather | solution.py:367
  89.8 1.1 copy-done.3
  90.9 1.1 copy-done.6
  92.1 1.1 copy-done.9
  93.2 8.1 %near_grad.1.near = f32[768,768]{1,0:T(8,128)} custom-call(bf16[8,2,192,768]{3,2,1,0:T(8,128)(2,1)} %bitcast.66, bf16[128,3072]{1,0:T(8,128)(2,1)S(1)} %copy-done.3, bf16[128,3072]{1,0:T(8,128)(2,1)} %collective-permute-done.5.refs_1_, bf16[128,3072]{1,0:T(8,128)(2,1)S(1)} %copy-done.6, bf16[128,3072]{1,0:T(8,128)(2,1)} %collective-permute-done.6.refs_3_, ...), custom_call_target="tpu_custom_call" | custom-call | flops 3623878656 | bytes 11796480 | tf_op jit(solution)/shard_map/near_grad/pallas_call | solution.py:218
  101.7 4.2 %pack.1 = (bf16[1024,768]{1,0:T(8,128)(2,1)S(1)}, bf16[1024,768]{1,0:T(8,128)(2,1)S(1)}) custom-call(s32[1,2048]{1,0:T(1,128)S(1)} %compare_select_fusion.8.place, bf16[16,136,768]{2,1,0:T(8,128)(2,1)S(1)} %all-to-all-done.incoming), custom_call_target="tpu_custom_call" | custom-call | flops 3221225472 | bytes 6291456 | tf_op jit(solution)/shard_map/pack/pallas_call | solution.py:126
  105.9 1.1 copy-done.1
  107.0 1.2 copy-done.10
  109.0 1.5 collective-permute-done.10.refs_8_.refs_2_
  111.0 9.0 %weight_grad.1 = bf16[8,2,192,768]{3,2,1,0:T(8,128)(2,1)} custom-call(bf16[1024,768]{1,0:T(8,128)(2,1)} %copy-done.10, bf16[128,3072]{1,0:T(8,128)(2,1)S(1)} %copy-done.4, bf16[128,3072]{1,0:T(8,128)(2,1)} %collective-permute-done.5.refs_1_, bf16[128,3072]{1,0:T(8,128)(2,1)S(1)} %copy-done.7, bf16[128,3072]{1,0:T(8,128)(2,1)} %collective-permute-done.6.refs_3_, ...), custom_call_target="tpu_custom_call" | custom-call | flops 4831838208 | bytes 12582912 | tf_op jit(solution)/shard_map/weight_grad/pallas_call | solution.py:158
  120.4 6.9 %hidden_grad.1.grad = bf16[1024,768]{1,0:T(8,128)(2,1)S(1)} custom-call(bf16[1024,768]{1,0:T(8,128)(2,1)} %copy-done.1, f32[768,768]{1,0:T(8,128)} %near_grad.1.near, bf16[8,2,192,768]{3,2,1,0:T(8,128)(2,1)} %bitcast.67, bf16[64,3072]{1,0:T(8,128)(2,1)} %collective-permute-done.8.refs_6_.refs_0_, bf16[64,3072]{1,0:T(8,128)(2,1)} %collective-permute-done.9.refs_7_.refs_1_, ...), custom_call_target="tpu_custom_call" | custom-call | flops 1207959552 | bytes 7077888 | tf_op jit(solution)/shard_map/hidden_grad/pallas_call | solution.py:265
  127.4 4.5 %unpack.1 = bf16[16,128,768]{2,1,0:T(8,128)(2,1)S(1)} custom-call(s32[2048,1]{1,0:T(8,128)S(1)} %copy.9.place, bf16[1024,768]{1,0:T(8,128)(2,1)S(1)} %hidden_grad.1.grad), custom_call_target="tpu_custom_call" | custom-call | flops 3221225472 | bytes 4718592 | tf_op jit(solution)/shard_map/unpack/pallas_call | solution.py:290
  131.9 1.7 copy-done
  133.5 7.1 %all-to-all-start.1 = ((bf16[16,128,768]{2,1,0:T(8,128)(2,1)}), bf16[16,128,768]{2,1,0:T(8,128)(2,1)S(1)}, u32[]{:S(2)}, u32[]{:S(2)}) async-start(bf16[16,128,768]{2,1,0:T(8,128)(2,1)} %copy-done), calls=%async_computation.1 | async-start | bytes 6291456 | tf_op jit(solution)/shard_map/all_to_all | solution.py:390
  140.6 41.8 %reduce-scatter.2.cloned.1.call-done = bf16[1,2,192,768]{3,2,1,0:T(8,128)(2,1)} async-done(((bf16[8,2,192,768]{3,2,1,0:T(8,128)(2,1)}), bf16[1,2,192,768]{3,2,1,0:T(8,128)(2,1)}) %reduce-scatter.2.cloned.1.call-update) | async-done | bytes 589840 | tf_op jit(solution)/shard_map/reduce_scatter | solution.py:386
  182.5 1.6 multiply_reduce_fusion
  184.1 1.3 collective-permute-start.12
  186.0 7.5 %all-to-all-start.2 = ((f32[32,1,192]{2,1,0:T(1,128)}), f32[32,1,192]{2,1,0:T(1,128)S(1)}, u32[]{:S(2)}, u32[]{:S(2)}) async-start(f32[32,1,192]{2,1,0:T(1,128)} %all_to_all.16), calls=%async_computation.3 | async-start | bytes 65536 | tf_op jit(solution)/shard_map/all_to_all | solution.py:399
  193.5 1.8 join_columns.1
  195.3 5.4 %all-to-all-done.2 = f32[32,1,192]{2,1,0:T(1,128)S(1)} async-done(((f32[32,1,192]{2,1,0:T(1,128)}), f32[32,1,192]{2,1,0:T(1,128)S(1)}, u32[]{:S(2)}, u32[]{:S(2)}) %all-to-all-start.2) | async-done | bytes 24608 | tf_op jit(solution)/shard_map/all_to_all | solution.py:399
  200.8 2.1 %fusion.1 = f32[768,192]{0,1:T(8,128)} fusion(f32[192,768]{1,0:T(8,128)} %get-tuple-element.50, bf16[192,768]{1,0:T(8,128)(2,1)} %collective-permute-done.12, bf16[1,2,192,768]{3,2,1,0:T(8,128)(2,1)} %reduce-scatter.2.cloned.1.call-done, s32[]{:T(128)S(6)} %select_n.218), kind=kLoop, calls=%fused_computation.4 | loop fusion | flops 589824 | bytes 1769476 | tf_op jit(solution)/shard_map/transpose | solution.py:402
  (65 shorter events, 12.0 us)
Async XLA Ops:
  7.2 82.6 %all-gather.3.cloned.1.call-start = ((), (), s32[]{:S(2)}) async-start(), calls=%async_computation.5 | async-start | bytes 5308416 | tf_op jit(solution)/shard_map/all_gather | solution.py:367
  7.2 12.8 %collective-permute-start = (bf16[64,3072]{1,0:T(8,128)(2,1)}, bf16[64,3072]{1,0:T(8,128)(2,1)S(1)}, u32[]{:S(2)}, u32[]{:S(2)}) collective-permute-start(bf16[64,3072]{1,0:T(8,128)(2,1)} %param.9), channel_id=1, source_target_pairs={{0,2},{2,0},{1,3},{3,1},{4,6},{6,4},{5,7},{7,5},{8,10},{10,8},{9,1... | collective-permute-start | bytes 1179656 | tf_op jit(solution)/shard_map/ppermute | solution.py:45
  14.9 11.5 %collective-permute-start.4 = (bf16[192,768]{1,0:T(8,128)(2,1)S(1)}, bf16[192,768]{1,0:T(8,128)(2,1)S(1)}, u32[]{:S(2)}, u32[]{:S(2)}) collective-permute-start(bf16[192,768]{1,0:T(8,128)(2,1)S(1)} %fusion.5), channel_id=1, source_target_pairs={{0,128},{128,0},{1,129},{129,1},{2,130},{130,2},{3,131},{131,3},{4... | collective-permute-start | bytes 884744 | tf_op jit(solution)/shard_map/ppermute | solution.py:45
  16.7 3.3 %copy-start.13 = (bf16[64,3072]{1,0:T(8,128)(2,1)S(1)}, bf16[64,3072]{1,0:T(8,128)(2,1)}, u32[]{:S(2)}) copy-start(bf16[64,3072]{1,0:T(8,128)(2,1)} %param.9) | copy-start | bytes 1179652
  20.0 10.2 %copy-start.12 = (bf16[768,192]{0,1:T(8,128)(2,1)S(1)}, bf16[768,192]{0,1:T(8,128)(2,1)}, u32[]{:S(2)}) copy-start(bf16[768,192]{0,1:T(8,128)(2,1)} %param.10) | copy-start | bytes 884740
  20.1 28.3 %copy-start.2 = (bf16[128,3072]{1,0:T(8,128)(2,1)}, bf16[128,3072]{1,0:T(8,128)(2,1)S(1)}, u32[]{:S(2)}) copy-start(bf16[128,3072]{1,0:T(8,128)(2,1)S(1)} %pad_maximum_fusion.refs_0_) | copy-start | bytes 2359300
  27.4 18.9 %collective-permute-start.1 = (bf16[128,3072]{1,0:T(8,128)(2,1)S(1)}, bf16[128,3072]{1,0:T(8,128)(2,1)S(1)}, u32[]{:S(2)}, u32[]{:S(2)}) collective-permute-start(bf16[128,3072]{1,0:T(8,128)(2,1)S(1)} %pad_maximum_fusion.refs_0_), channel_id=1, source_target_pairs={{0,4},{4,8},{8,12},{12,0},{1,5},{5,9},{9,13},{13,1},{2,6},{6,10},{... | collective-permute-start | bytes 2359304 | tf_op jit(solution)/shard_map/ppermute | solution.py:50
  28.7 18.4 %collective-permute-start.2 = (bf16[128,3072]{1,0:T(8,128)(2,1)S(1)}, bf16[128,3072]{1,0:T(8,128)(2,1)S(1)}, u32[]{:S(2)}, u32[]{:S(2)}) collective-permute-start(bf16[128,3072]{1,0:T(8,128)(2,1)S(1)} %pad_maximum_fusion.refs_0_), channel_id=1, source_target_pairs={{0,12},{4,0},{8,4},{12,8},{1,13},{5,1},{9,5},{13,9},{2,14},{6,2},{... | collective-permute-start | bytes 2359304 | tf_op jit(solution)/shard_map/ppermute | solution.py:50
  33.6 14.6 %copy-start.11 = (f32[192,768]{1,0:T(8,128)}, f32[192,768]{1,0:T(8,128)S(1)}, u32[]{:S(2)}) copy-start(f32[192,768]{1,0:T(8,128)S(1)} %get-tuple-element.38) | copy-start | bytes 1769476
  33.6 14.8 %collective-permute-start.3 = (f32[192,768]{1,0:T(8,128)S(1)}, f32[192,768]{1,0:T(8,128)}, u32[]{:S(2)}, u32[]{:S(2)}) collective-permute-start(f32[192,768]{1,0:T(8,128)S(1)} %get-tuple-element.38), channel_id=1, source_target_pairs={{0,128},{128,0},{1,129},{129,1},{2,130},{130,2},{3,131},{131,3},{4... | collective-permute-start | bytes 1769480 | tf_op jit(solution)/shard_map/ppermute | solution.py:45
  46.3 1.0 copy-start.5
  47.3 1.0 copy-start.8
  48.3 53.0 %all-to-all-start = ((bf16[16,136,768]{2,1,0:T(8,128)(2,1)}), bf16[16,136,768]{2,1,0:T(8,128)(2,1)S(1)}, u32[]{:S(2)}, u32[]{:S(2)}) async-start(bf16[16,136,768]{2,1,0:T(8,128)(2,1)} %split_columns.1), calls=%async_computation | async-start | bytes 6684672 | tf_op jit(solution)/shard_map/all_to_all | solution.py:375
  55.2 127.2 %reduce-scatter.2.cloned.1.call-start = ((), (), s32[]{:S(2)}) async-start(), calls=%async_computation.4 | async-start | bytes 5308416 | tf_op jit(solution)/shard_map/reduce_scatter | solution.py:386
  55.3 3.6 %collective-permute-start.5 = (bf16[128,3072]{1,0:T(8,128)(2,1)}, bf16[128,3072]{1,0:T(8,128)(2,1)}, u32[]{:S(2)}, u32[]{:S(2)}) collective-permute-start(bf16[128,3072]{1,0:T(8,128)(2,1)} %copy-done.2), channel_id=1, source_target_pairs={{0,1},{1,0},{2,3},{3,2},{4,5},{5,4},{6,7},{7,6},{8,9},{9,8},{10,11... | collective-permute-start | bytes 2359304 | tf_op jit(solution)/shard_map/ppermute | solution.py:45
  55.5 3.6 %collective-permute-start.6 = (bf16[128,3072]{1,0:T(8,128)(2,1)}, bf16[128,3072]{1,0:T(8,128)(2,1)}, u32[]{:S(2)}, u32[]{:S(2)}) collective-permute-start(bf16[128,3072]{1,0:T(8,128)(2,1)} %copy-done.5), channel_id=1, source_target_pairs={{0,1},{1,0},{2,3},{3,2},{4,5},{5,4},{6,7},{7,6},{8,9},{9,8},{10,11... | collective-permute-start | bytes 2359304 | tf_op jit(solution)/shard_map/ppermute | solution.py:45
  55.9 4.4 %collective-permute-start.7 = (bf16[128,3072]{1,0:T(8,128)(2,1)}, bf16[128,3072]{1,0:T(8,128)(2,1)}, u32[]{:S(2)}, u32[]{:S(2)}) collective-permute-start(bf16[128,3072]{1,0:T(8,128)(2,1)} %copy-done.8), channel_id=1, source_target_pairs={{0,1},{1,0},{2,3},{3,2},{4,5},{5,4},{6,7},{7,6},{8,9},{9,8},{10,11... | collective-permute-start | bytes 2359304 | tf_op jit(solution)/shard_map/ppermute | solution.py:45
  56.0 52.2 %collective-permute-start.8 = (bf16[64,3072]{1,0:T(8,128)(2,1)}, bf16[64,3072]{1,0:T(8,128)(2,1)}, u32[]{:S(2)}, u32[]{:S(2)}) collective-permute-start(bf16[64,3072]{1,0:T(8,128)(2,1)} %slice.36), channel_id=1, source_target_pairs={{0,4},{4,8},{8,12},{12,0},{1,5},{5,9},{9,13},{13,1},{2,6},{6,10},{... | collective-permute-start | bytes 1179656 | tf_op jit(solution)/shard_map/ppermute | solution.py:50
  57.6 50.6 %collective-permute-start.9 = (bf16[64,3072]{1,0:T(8,128)(2,1)}, bf16[64,3072]{1,0:T(8,128)(2,1)}, u32[]{:S(2)}, u32[]{:S(2)}) collective-permute-start(bf16[64,3072]{1,0:T(8,128)(2,1)} %slice.37), channel_id=1, source_target_pairs={{0,12},{4,0},{8,4},{12,8},{1,13},{5,1},{9,5},{13,9},{2,14},{6,2},{... | collective-permute-start | bytes 1179656 | tf_op jit(solution)/shard_map/ppermute | solution.py:50
  89.8 1.1 copy-start.3
  90.9 1.1 copy-start.6
  92.1 1.1 copy-start.9
  101.7 9.3 %copy-start.4 = (bf16[128,3072]{1,0:T(8,128)(2,1)S(1)}, bf16[128,3072]{1,0:T(8,128)(2,1)}, u32[]{:S(2)}) copy-start(bf16[128,3072]{1,0:T(8,128)(2,1)} %copy-done.2) | copy-start | bytes 2359300
  101.7 9.3 %copy-start.7 = (bf16[128,3072]{1,0:T(8,128)(2,1)S(1)}, bf16[128,3072]{1,0:T(8,128)(2,1)}, u32[]{:S(2)}) copy-start(bf16[128,3072]{1,0:T(8,128)(2,1)} %copy-done.5) | copy-start | bytes 2359300
  105.9 1.2 copy-start.1
  107.0 1.2 copy-start.10
  108.2 2.2 %collective-permute-start.10 = (bf16[64,3072]{1,0:T(8,128)(2,1)}, bf16[64,3072]{1,0:T(8,128)(2,1)S(1)}, u32[]{:S(2)}, u32[]{:S(2)}) collective-permute-start(bf16[64,3072]{1,0:T(8,128)(2,1)} %collective-permute-done.8.refs_6_.refs_0_), channel_id=1, source_target_pairs={{0,1},{1,0},{2,3},{3,2},{4,5},{5,4},{6,7},{7,6},{8,9},{9,8},{10,11... | collective-permute-start | bytes 1179656 | tf_op jit(solution)/shard_map/ppermute | solution.py:45
  108.9 2.1 %collective-permute-start.11 = (bf16[64,3072]{1,0:T(8,128)(2,1)}, bf16[64,3072]{1,0:T(8,128)(2,1)S(1)}, u32[]{:S(2)}, u32[]{:S(2)}) collective-permute-start(bf16[64,3072]{1,0:T(8,128)(2,1)} %collective-permute-done.9.refs_7_.refs_1_), channel_id=1, source_target_pairs={{0,1},{1,0},{2,3},{3,2},{4,5},{5,4},{6,7},{7,6},{8,9},{9,8},{10,11... | collective-permute-start | bytes 1179656 | tf_op jit(solution)/shard_map/ppermute | solution.py:45
  131.9 1.7 copy-start
  133.5 51.8 %all-to-all-start.1 = ((bf16[16,128,768]{2,1,0:T(8,128)(2,1)}), bf16[16,128,768]{2,1,0:T(8,128)(2,1)S(1)}, u32[]{:S(2)}, u32[]{:S(2)}) async-start(bf16[16,128,768]{2,1,0:T(8,128)(2,1)} %copy-done), calls=%async_computation.1 | async-start | bytes 6291456 | tf_op jit(solution)/shard_map/all_to_all | solution.py:390
  184.1 16.7 %collective-permute-start.12 = (bf16[192,768]{1,0:T(8,128)(2,1)S(1)}, bf16[192,768]{1,0:T(8,128)(2,1)}, u32[]{:S(2)}, u32[]{:S(2)}) collective-permute-start(bf16[192,768]{1,0:T(8,128)(2,1)S(1)} %get-tuple-element.54), channel_id=1, source_target_pairs={{0,128},{128,0},{1,129},{129,1},{2,130},{130,2},{3,131},{131,3},{4... | collective-permute-start | bytes 884744 | tf_op jit(solution)/shard_map/ppermute | solution.py:45
  186.0 14.7 %all-to-all-start.2 = ((f32[32,1,192]{2,1,0:T(1,128)}), f32[32,1,192]{2,1,0:T(1,128)S(1)}, u32[]{:S(2)}, u32[]{:S(2)}) async-start(f32[32,1,192]{2,1,0:T(1,128)} %all_to_all.16), calls=%async_computation.3 | async-start | bytes 65536 | tf_op jit(solution)/shard_map/all_to_all | solution.py:399
Sparse Core Ops, SparseCore 0:
  27.5 62.2 all-gather.2
  120.2 62.2 reduce-scatter.1

commit v4 on v3

--- a/solution.py
+++ b/solution.py
@@ -22,6 +22,12 @@
 SWAP = [(0, 1), (1, 0)]
 
 ON_CHIP = pl.BlockSpec(memory_space=pltpu.VMEM)
+
+
+def vmem(mebibytes):
+    return pltpu.CompilerParams(vmem_limit_bytes=mebibytes * 1024 * 1024)
+
+
 LARGE_VMEM = pltpu.CompilerParams(vmem_limit_bytes=50 * 1024 * 1024)
 SMALL_VMEM = pltpu.CompilerParams(vmem_limit_bytes=24 * 1024 * 1024)
 
@@ -93,7 +99,7 @@
         in_specs=[ON_CHIP],
         out_specs=pl.BlockSpec((rows, many * width), lambda i: (0, i)),
         out_shape=jax.ShapeDtypeStruct((rows, count * width), values.dtype),
-        compiler_params=SMALL_VMEM,
+        compiler_params=vmem(24),
         cost_estimate=pl.CostEstimate(
             flops=0, bytes_accessed=4 * values.size, transcendentals=0
         ),
@@ -107,7 +113,7 @@
     )
 
 
-def pack_body(place, incoming, packed, act):
+def pack_body(place, incoming, packed, act, token):
     part, hidden = 256, packed.shape[1]
     slots = place.shape[1]
     each = slots // incoming.shape[0]
@@ -118,6 +124,7 @@
     found = jnp.dot(pick, source, preferred_element_type=jnp.float32)
     packed[pl.ds(start, part), :] = narrow(found)
     act[pl.ds(start, part), :] = narrow(gelu_pair(found)[0])
+    token[...] = found[:8, :128]
 
 
 def pack(place, incoming, rows):
@@ -127,9 +134,10 @@
         pack_body,
         grid=(rows // 256,),
         in_specs=[pl.BlockSpec((1, slots), lambda i: (0, 0)), ON_CHIP],
-        out_specs=[ON_CHIP, ON_CHIP],
-        out_shape=[jax.ShapeDtypeStruct((rows, hidden), jnp.bfloat16)] * 2,
-        compiler_params=SMALL_VMEM,
+        out_specs=[ON_CHIP, ON_CHIP, pl.BlockSpec((8, 128), lambda i: (0, 0))],
+        out_shape=[jax.ShapeDtypeStruct((rows, hidden), jnp.bfloat16)] * 2
+        + [jax.ShapeDtypeStruct((8, 128), jnp.float32)],
+        compiler_params=vmem(40),
         cost_estimate=pl.CostEstimate(
             flops=2 * rows * hidden * slots,
             bytes_accessed=2 * slots * hidden + 4 * rows * hidden,
@@ -164,7 +172,7 @@
             (deep, 1, width, hidden), lambda i: (i % around, i // around, 0, 0)
         ),
         out_shape=jax.ShapeDtypeStruct((count, sides, width, hidden), jnp.bfloat16),
-        compiler_params=LARGE_VMEM,
+        compiler_params=vmem(52),
         cost_estimate=pl.CostEstimate(
             flops=2 * rows * hidden * outputs,
             bytes_accessed=2 * rows * (outputs + hidden) + 2 * outputs * hidden,
@@ -174,105 +182,61 @@
     )(act, *pieces)
 
 
-def near_grad_body(weight, *refs):
-    pieces, total = refs[:-1], refs[-1]
+def hidden_grad_body(steps, packed, weight, *refs):
+    pieces, (out, slope, total) = refs[:-3], refs[-3:]
     step = pl.program_id(0)
-    tile = weight.shape[0] * weight.shape[2]
+
+    part = slope.shape[0] // steps
+    some = pl.ds(pl.multiple_of(step * part, part), part)
+    slope[some, :] = gelu_pair(wide(packed[some, :]))[1]
+
     grads = stacked(pieces)
-    block = weight[...].reshape(tile, total.shape[1])
+    block = weight[...].reshape(grads.shape[1], total.shape[1])
     grad = jnp.dot(grads, block, preferred_element_type=jnp.float32)
 
     @pl.when(step == 0)
     def _():
         total[...] = grad
 
-    @pl.when(step > 0)
+    @pl.when((step > 0) & (step < steps - 1))
     def _():
         total[...] += grad
 
-
-def hidden_specs(pieces, weight, steps):
-    tile = pieces[0].shape[1] // steps
+    @pl.when(step == steps - 1)
+    def _():
+        out[...] = narrow((total[...] + grad) * slope[...])
+
+
+def hidden_grad(packed, pieces, weight):
+    rows = sum(piece.shape[0] for piece in pieces)
+    outputs = pieces[0].shape[1]
+    steps = 4
+    tile = outputs // steps
     count, sides, width, hidden = weight.shape
     deep = tile // width
     around = count // deep
-    return [
-        pl.BlockSpec((deep, 1, width, hidden), lambda i: (i % around, i // around, 0, 0)),
-    ] + [pl.BlockSpec((piece.shape[0], tile), lambda i: (0, i)) for piece in pieces]
-
-
-def hidden_cost(rows, weight, transcendentals):
-    hidden = weight.shape[-1]
-    outputs = weight.size // hidden
-    return pl.CostEstimate(
-        flops=2 * rows * hidden * outputs,
-        bytes_accessed=2 * rows * outputs + 2 * outputs * hidden + 4 * rows * hidden,
-        transcendentals=transcendentals,
-    )
-
-
-def near_grad(pieces, weight):
-    rows = sum(piece.shape[0] for piece in pieces)
-    hidden = weight.shape[-1]
-    steps = 4
-    return pl.pallas_call(
-        near_grad_body,
-        grid=(steps,),
-        in_specs=hidden_specs(pieces, weight, steps),
-        out_specs=ON_CHIP,
-        out_shape=jax.ShapeDtypeStruct((rows, hidden), jnp.float32),
-        compiler_params=LARGE_VMEM,
-        cost_estimate=hidden_cost(rows, weight, 0),
-        name="near_grad",
-    )(weight, *pieces)
-
-
-def hidden_grad_body(steps, packed, near, weight, *refs):
-    pieces, (out, total) = refs[:-2], refs[-2:]
-    step = pl.program_id(0)
-    rows = near.shape[0]
-
-    def slope(some):
-        return gelu_pair(wide(packed[some, :]))[1]
-
-    part = rows // steps
-    some = pl.ds(pl.multiple_of(step * part, part), part)
-    out[some, :] = narrow(near[some, :] * slope(some))
-
-    tile = weight.shape[0] * weight.shape[2]
-    grads = stacked(pieces)
-    block = weight[...].reshape(tile, total.shape[1])
-    grad = jnp.dot(grads, block, preferred_element_type=jnp.float32)
-
-    @pl.when(step == 0)
-    def _():
-        total[...] = grad
-
-    @pl.when((step > 0) & (step < steps - 1))
-    def _():
-        total[...] += grad
-
-    @pl.when(step == steps - 1)
-    def _():
-        rest = pl.ds(rows, total.shape[0])
-        out[rest, :] = narrow((total[...] + grad) * slope(rest))
-
-
-def hidden_grad(packed, near, pieces, weight):
-    rows = sum(piece.shape[0] for piece in pieces)
-    total, hidden = near.shape[0] + rows, weight.shape[-1]
-    steps = 4
     return pl.pallas_call(
         functools.partial(hidden_grad_body, steps),
         grid=(steps,),
-        in_specs=[ON_CHIP, ON_CHIP] + hidden_specs(pieces, weight, steps),
-        out_specs=ON_CHIP,
-        out_shape=jax.ShapeDtypeStruct((total, hidden), jnp.bfloat16),
-        scratch_shapes=[pltpu.VMEM((rows, hidden), jnp.float32)],
-        compiler_params=LARGE_VMEM,
-        cost_estimate=hidden_cost(rows, weight, total * hidden),
+        in_specs=[
+            pl.BlockSpec((rows, hidden), lambda i: (0, 0), pipeline_mode=pl.Buffered(1)),
+            pl.BlockSpec((deep, 1, width, hidden), lambda i: (i % around, i // around, 0, 0)),
+        ]
+        + [pl.BlockSpec((piece.shape[0], tile), lambda i: (0, i)) for piece in pieces],
+        out_specs=pl.BlockSpec((rows, hidden), lambda i: (0, 0)),
+        out_shape=jax.ShapeDtypeStruct((rows, hidden), jnp.bfloat16),
+        scratch_shapes=[
+            pltpu.VMEM((rows, hidden), jnp.float32),
+            pltpu.VMEM((rows, hidden), jnp.float32),
+        ],
+        compiler_params=vmem(54),
+        cost_estimate=pl.CostEstimate(
+            flops=2 * rows * hidden * outputs,
+            bytes_accessed=2 * rows * outputs + 2 * outputs * hidden + 4 * rows * hidden,
+            transcendentals=rows * hidden,
+        ),
         name="hidden_grad",
-    )(packed, near, weight, *pieces)
+    )(packed, weight, *pieces)
 
 
 def unpack_body(place, grad, out):
@@ -298,7 +262,7 @@
             (owners // steps, slots // owners, hidden), lambda i: (i, 0, 0)
         ),
         out_shape=jax.ShapeDtypeStruct((owners, slots // owners, hidden), jnp.bfloat16),
-        compiler_params=SMALL_VMEM,
+        compiler_params=vmem(54),
         cost_estimate=pl.CostEstimate(
             flops=2 * rows * hidden * slots,
             bytes_accessed=2 * slots * hidden + 2 * rows * hidden,
@@ -362,30 +326,27 @@
     latent = wide(latent_weight.T)
     weight = narrow(step_column * soft_quantize(latent, step_column)[0])
     weight = lax.optimization_barrier(weight)
-    other = after(swap(weight, "a"), near[0])
+    other = after(swap(weight, "a"), near[2], near[4])
     weight = jnp.stack([jnp.where(a == 0, weight, other), jnp.where(a == 0, other, weight)])
     weight = lax.all_gather(weight, "z", axis=0)
 
-    latent = wide(after(latent_weight, near[0]).T)
+    latent = wide(after(latent_weight, near[2], near[4]).T)
     quantized, slope, ratio = soft_quantize(latent, step_column)
     slope, pull = lax.optimization_barrier((slope, quantized - ratio * slope))
     pull_other = swap(pull, "a")
 
-    outgoing = after(outgoing, *ends, pull_other)
+    outgoing = after(outgoing, *ends)
     incoming = lax.all_to_all(outgoing, DP, split_axis=0, concat_axis=0, tiled=True)
-    near_part = near_grad(near, weight)
-    incoming, near_part = lax.optimization_barrier((incoming, near_part))
-
     codes = incoming[:, capacity, : 2 * capacity].astype(jnp.int32)
     slots = codes[:, :capacity] * 32 + codes[:, capacity:]
     place = places(slots.reshape(16 * capacity), block)
-    packed, act = pack(place.reshape(1, -1), incoming, 16 * block)
-    far = gather_far(ends, act)
-    column = after(place, act).reshape(-1, 1)
+    packed, act, token = pack(place.reshape(1, -1), incoming, 16 * block)
+    far = gather_far(ends, token)
+    column = after(place, token).reshape(-1, 1)
     partial = weight_grad(after(act, column), near + far, 8, 2, width)
     summed = lax.psum_scatter(partial, "z", scatter_dimension=0, tiled=True)[0]
 
-    grad = hidden_grad(after(packed, partial), near_part, far, weight)
+    grad = hidden_grad(packed, near + far, after(weight, partial, pull_other))
     picked = unpack(column, grad, 16)
     returned = lax.all_to_all(picked, DP, split_axis=0, concat_axis=0, tiled=True)
     grad_acts = join_columns(returned)

time: 211 us -> 229 us (1.085)
  waiting for transfers between devices: 98.4 us -> 111 us
  starting transfers between devices: 35.3 us -> 46 us
  local copies, waits for them, and re-layouts: 10.5 us -> 6.82 us
    all_to_all x1, waiting for transfers between devices: 0.01 us -> 38.3 us  [shards(): lax.all_to_all(outgoing, DP, split_axis=0, concat_axis=0, tiled=True)]
    all_gather x1, waiting for transfers between devices: 29.6 us -> 0.01 us  [shards(): weight = lax.all_gather(weight, 'z', axis=0)]
    reduce_scatter x1, waiting for transfers between devices: 41.8 us -> 17.2 us  [shards(): summed = lax.psum_scatter(partial, 'z', scatter_dimension=0, tiled=True)[0]]
    all_to_all x1, waiting for transfers between devices: 0.01 us -> 19.8 us  [shards(): lax.all_to_all(picked, DP, split_axis=0, concat_axis=0, tiled=True)]
    ppermute x9, waiting for transfers between devices: 9.85 us -> 23.1 us  [swap(): return lax.ppermute(value, axis, SWAP)]
    pallas_call x1 -> x0, Pallas kernels: 8.13 us -> none  [near_grad(): pl.pallas_call(near_grad_body, grid=(steps,), in_specs=hidden_specs(piece...]
    pallas_call x1, Pallas kernels: 6.9 us -> 11.7 us  [hidden_grad(): pl.pallas_call(functools.partial(hidden_grad_body, steps), grid=(steps,),...]
    ppermute x4, waiting for transfers between devices: 11.7 us -> 7.11 us  [shift(): lax.ppermute(value, axis, [(i, (i + by) % count) for i in range(count)])]
  transfers between devices with their start and end apart: 18 -> 18, of which waited for: 9 -> 11; matrix products, arithmetic and copies ran while one was open for 6% -> 5% of each run, Pallas kernels for 14% -> 16%
where the time goes in v4:
time: 229 us; the launch traced here: 228 us
  waiting for transfers between devices  111 us (48%)
  starting transfers between devices  46 us (20%)
  Pallas kernels  37.3 us (16%)
  between operations  14.2 us (6%)
  other arithmetic  12.8 us (6%)
  local copies, waits for them, and re-layouts  6.82 us (3%)
    all_to_all x1, waiting for transfers between devices, shards(): lax.all_to_all(outgoing, DP, split_axis=0, concat_axis=0, tiled=True)  38.3 us
    ppermute x9, waiting for transfers between devices, swap(): return lax.ppermute(value, axis, SWAP)  23.1 us
    all_to_all x1, waiting for transfers between devices, shards(): lax.all_to_all(picked, DP, split_axis=0, concat_axis=0, tiled=True)  19.8 us
    reduce_scatter x1, waiting for transfers between devices, shards(): summed = lax.psum_scatter(partial, 'z', scatter_dimension=0, tiled=True)[0]  17.2 us
    pallas_call x1, Pallas kernels, hidden_grad(): pl.pallas_call(functools.partial(hidden_grad_body, steps), grid=(steps,),...  11.7 us
    all_to_all x1, starting transfers between devices, shards(): lax.all_to_all(picked, DP, split_axis=0, concat_axis=0, tiled=True)  11.5 us
    all_to_all x1, starting transfers between devices, shards(): lax.all_to_all(outgoing, DP, split_axis=0, concat_axis=0, tiled=True)  9.58 us
    all_to_all x1, starting transfers between devices, shards(): lax.all_to_all(shares, ('a',) + DP, split_axis=0, concat_axis=0, tiled=True)  9.54 us
  transfers between devices with their start and end apart: 18, of which 11 were waited for; matrix products, arithmetic and copies ran while one was open for 5% of the time, Pallas kernels for 16%

profile of v4, /device:TPU:1, one launch (start us, length us, event | category | flops | bytes accessed | tf_op | source)
XLA Modules:
  0.0 228.0 jit_solution(18204459916823220022)
XLA Ops:
  7.2 3.8 %collective-permute-start = (bf16[64,3072]{1,0:T(8,128)(2,1)}, bf16[64,3072]{1,0:T(8,128)(2,1)S(1)}, u32[]{:S(2)}, u32[]{:S(2)}) collective-permute-start(bf16[64,3072]{1,0:T(8,128)(2,1)} %param.9), channel_id=1, source_target_pairs={{0,2},{2,0},{1,3},{3,1},{4,6},{6,4},{5,7},{7,5},{8,10},{10,8},{9,1... | collective-permute-start | bytes 1179656 | tf_op jit(solution)/shard_map/ppermute | solution.py:51
  12.3 3.3 %split_columns.1 = bf16[16,136,768]{2,1,0:T(8,128)(2,1)} custom-call(bf16[128,12288]{1,0:T(8,128)(2,1)} %source.1, bf16[8,768]{1,0:T(8,128)(2,1)} %fusion.11.codes), custom_call_target="tpu_custom_call" | custom-call | bytes 6291456 | tf_op jit(solution)/shard_map/split_columns/pallas_call | solution.py:70
  15.6 3.5 %collective-permute-done = bf16[64,3072]{1,0:T(8,128)(2,1)S(1)} collective-permute-done((bf16[64,3072]{1,0:T(8,128)(2,1)}, bf16[64,3072]{1,0:T(8,128)(2,1)S(1)}, u32[]{:S(2)}, u32[]{:S(2)}) %collective-permute-start) | collective-permute-done | bytes 393248 | tf_op jit(solution)/shard_map/ppermute | solution.py:51
  19.2 2.0 collective-permute-start.1
  21.2 1.4 collective-permute-start.2
  22.5 2.3 %fusion.5 = bf16[192,768]{1,0:T(8,128)(2,1)S(1)} fusion(bf16[768,192]{0,1:T(8,128)(2,1)S(1)} %copy-done.5, f32[192]{0:T(256)S(1)} %bitcast.70), kind=kLoop, calls=%fused_computation.15 | loop fusion | flops 1327104 | bytes 590592 | tf_op jit(solution)/shard_map/convert_element_type | solution.py:302
  24.9 1.5 collective-permute-start.3
  26.4 4.9 %collective-permute-done.3 = bf16[192,768]{1,0:T(8,128)(2,1)S(1)} collective-permute-done((bf16[192,768]{1,0:T(8,128)(2,1)S(1)}, bf16[192,768]{1,0:T(8,128)(2,1)S(1)}, u32[]{:S(2)}, u32[]{:S(2)}) %collective-permute-start.3) | collective-permute-done | bytes 294944 | tf_op jit(solution)/shard_map/ppermute | solution.py:51
  31.3 7.0 %collective-permute-done.1.refs_2_ = bf16[128,3072]{1,0:T(8,128)(2,1)S(1)} collective-permute-done((bf16[128,3072]{1,0:T(8,128)(2,1)S(1)}, bf16[128,3072]{1,0:T(8,128)(2,1)S(1)}, u32[]{:S(2)}, u32[]{:S(2)}) %collective-permute-start.1) | collective-permute-done | bytes 786464 | tf_op jit(solution)/shard_map/ppermute | solution.py:56
  41.1 9.6 %all-to-all-start = ((bf16[16,136,768]{2,1,0:T(8,128)(2,1)}), bf16[16,136,768]{2,1,0:T(8,128)(2,1)S(1)}, u32[]{:S(2)}, u32[]{:S(2)}) async-start(bf16[16,136,768]{2,1,0:T(8,128)(2,1)} %split_columns.1), calls=%async_computation | async-start | bytes 6684672 | tf_op jit(solution)/shard_map/all_to_all | solution.py:339
  50.9 1.6 collective-permute-start.7
  52.5 1.2 collective-permute-start.8
  54.5 38.3 %all-to-all-done.incoming = bf16[16,136,768]{2,1,0:T(8,128)(2,1)S(1)} async-done(((bf16[16,136,768]{2,1,0:T(8,128)(2,1)}), bf16[16,136,768]{2,1,0:T(8,128)(2,1)S(1)}, u32[]{:S(2)}, u32[]{:S(2)}) %all-to-all-start) | async-done | bytes 3342368 | tf_op jit(solution)/shard_map/all_to_all | solution.py:339
  93.1 4.2 %pack.1 = (bf16[1024,768]{1,0:T(8,128)(2,1)S(1)}, bf16[1024,768]{1,0:T(8,128)(2,1)S(1)}, f32[8,128]{1,0:T(8,128)}) custom-call(s32[1,2048]{1,0:T(1,128)S(1)} %compare_select_fusion.8.place, bf16[16,136,768]{2,1,0:T(8,128)(2,1)S(1)} %all-to-all-done.incoming), custom_call_target="tpu_custom_call" | custom-call | flops 3221225472 | bytes 6291456 | tf_op jit(solution)/shard_map/pack/pallas_call | solution.py:133
  97.3 1.1 copy-done.2
  98.5 1.2 copy-done.3
  100.9 1.3 collective-permute-done.10.refs_9_
  102.7 9.4 %weight_grad.1 = bf16[8,2,192,768]{3,2,1,0:T(8,128)(2,1)} custom-call(bf16[1024,768]{1,0:T(8,128)(2,1)} %copy-done.3, bf16[128,3072]{1,0:T(8,128)(2,1)} %copy-done.7, bf16[128,3072]{1,0:T(8,128)(2,1)} %collective-permute-done.4.refs_1_, bf16[128,3072]{1,0:T(8,128)(2,1)} %copy-done.10, bf16[128,3072]{1,0:T(8,128)(2,1)} %collective-permute-done.5.refs_3_, ...), custom_call_target="tpu_custom_call" | custom-call | flops 4831838208 | bytes 12582912 | tf_op jit(solution)/shard_map/weight_grad/pallas_call | solution.py:166
  113.0 3.4 %fusion.4 = (f32[192,768]{1,0:T(8,128)S(1)}, f32[192,768]{1,0:T(8,128)}) fusion(bf16[768,192]{0,1:T(8,128)(2,1)S(1)} %copy-done.6, f32[192]{0:T(256)S(1)} %bitcast.71), kind=kLoop, calls=%fused_computation.10 | loop fusion | flops 2064384 | bytes 1475328 | tf_op jit(solution)/shard_map/sub | solution.py:335
  116.8 1.3 copy.9.place
  118.2 12.8 %collective-permute-done.11 = f32[192,768]{1,0:T(8,128)S(1)} collective-permute-done((f32[192,768]{1,0:T(8,128)S(1)}, f32[192,768]{1,0:T(8,128)S(1)}, u32[]{:S(2)}, u32[]{:S(2)}) %collective-permute-start.11) | collective-permute-done | bytes 589856 | tf_op jit(solution)/shard_map/ppermute | solution.py:51
  131.0 11.7 %hidden_grad.1.grad = bf16[1024,768]{1,0:T(8,128)(2,1)} custom-call(bf16[1024,768]{1,0:T(8,128)(2,1)} %copy-done.2, bf16[8,2,192,768]{3,2,1,0:T(8,128)(2,1)} %bitcast.75, bf16[128,3072]{1,0:T(8,128)(2,1)} %copy-done.7, bf16[128,3072]{1,0:T(8,128)(2,1)} %collective-permute-done.4.refs_1_, bf16[128,3072]{1,0:T(8,128)(2,1)} %copy-done.10, ...), custom_call_target="tpu_custom_call" | custom-call | flops 4831838208 | bytes 14155776 | tf_op jit(solution)/shard_map/hidden_grad/pallas_call | solution.py:218
  142.7 7.0 %unpack.1 = bf16[16,128,768]{2,1,0:T(8,128)(2,1)} custom-call(s32[2048,1]{1,0:T(8,128)} %copy.9.place, bf16[1024,768]{1,0:T(8,128)(2,1)} %hidden_grad.1.grad), custom_call_target="tpu_custom_call" | custom-call | flops 3221225472 | bytes 4718592 | tf_op jit(solution)/shard_map/unpack/pallas_call | solution.py:254
  149.7 11.5 %all-to-all-start.1 = ((bf16[16,128,768]{2,1,0:T(8,128)(2,1)}), bf16[16,128,768]{2,1,0:T(8,128)(2,1)S(1)}, u32[]{:S(2)}, u32[]{:S(2)}) async-start(bf16[16,128,768]{2,1,0:T(8,128)(2,1)} %unpack.1), calls=%async_computation.1 | async-start | bytes 6291456 | tf_op jit(solution)/shard_map/all_to_all | solution.py:351
  161.1 17.2 %reduce-scatter.2.cloned.1.call-done = bf16[1,2,192,768]{3,2,1,0:T(8,128)(2,1)} async-done(((bf16[8,2,192,768]{3,2,1,0:T(8,128)(2,1)}), bf16[1,2,192,768]{3,2,1,0:T(8,128)(2,1)}) %reduce-scatter.2.cloned.1.call-update) | async-done | bytes 589840 | tf_op jit(solution)/shard_map/reduce_scatter | solution.py:347
  178.4 1.6 multiply_reduce_fusion
  180.0 1.3 collective-permute-start.12
  181.3 19.8 %all-to-all-done.1.source = bf16[16,128,768]{2,1,0:T(8,128)(2,1)S(1)} async-done(((bf16[16,128,768]{2,1,0:T(8,128)(2,1)}), bf16[16,128,768]{2,1,0:T(8,128)(2,1)S(1)}, u32[]{:S(2)}, u32[]{:S(2)}) %all-to-all-start.1) | async-done | bytes 3145760 | tf_op jit(solution)/shard_map/all_to_all | solution.py:351
  201.7 9.5 %all-to-all-start.2 = ((f32[32,1,192]{2,1,0:T(1,128)}), f32[32,1,192]{2,1,0:T(1,128)S(1)}, u32[]{:S(2)}, u32[]{:S(2)}) async-start(f32[32,1,192]{2,1,0:T(1,128)} %all_to_all.16), calls=%async_computation.3 | async-start | bytes 65536 | tf_op jit(solution)/shard_map/all_to_all | solution.py:360
  211.2 1.8 join_columns.1
  213.0 5.4 %all-to-all-done.2 = f32[32,1,192]{2,1,0:T(1,128)S(1)} async-done(((f32[32,1,192]{2,1,0:T(1,128)}), f32[32,1,192]{2,1,0:T(1,128)S(1)}, u32[]{:S(2)}, u32[]{:S(2)}) %all-to-all-start.2) | async-done | bytes 24608 | tf_op jit(solution)/shard_map/all_to_all | solution.py:360
  218.5 2.1 fusion.1
  (62 shorter events, 9.9 us)
Async XLA Ops:
  7.2 123.8 %all-gather.3.cloned.1.call-start = ((), (), s32[]{:S(2)}) async-start(), calls=%async_computation.5 | async-start | bytes 5308416 | tf_op jit(solution)/shard_map/all_gather | solution.py:331
  7.2 11.9 %collective-permute-start = (bf16[64,3072]{1,0:T(8,128)(2,1)}, bf16[64,3072]{1,0:T(8,128)(2,1)S(1)}, u32[]{:S(2)}, u32[]{:S(2)}) collective-permute-start(bf16[64,3072]{1,0:T(8,128)(2,1)} %param.9), channel_id=1, source_target_pairs={{0,2},{2,0},{1,3},{3,1},{4,6},{6,4},{5,7},{7,5},{8,10},{10,8},{9,1... | collective-permute-start | bytes 1179656 | tf_op jit(solution)/shard_map/ppermute | solution.py:51
  12.3 6.8 %copy-start.9 = (bf16[64,3072]{1,0:T(8,128)(2,1)S(1)}, bf16[64,3072]{1,0:T(8,128)(2,1)}, u32[]{:S(2)}) copy-start(bf16[64,3072]{1,0:T(8,128)(2,1)} %param.9) | copy-start | bytes 1179652
  12.3 10.2 %copy-start.12 = (bf16[1,192]{1,0:T(2,128)(2,1)S(1)}, bf16[1,192]{1,0:T(2,128)(2,1)}, u32[]{:S(2)}) copy-start(bf16[1,192]{1,0:T(2,128)(2,1)} %param.11) | copy-start | bytes 1156
  12.3 10.2 %copy-start.5 = (bf16[768,192]{0,1:T(8,128)(2,1)S(1)}, bf16[768,192]{0,1:T(8,128)(2,1)}, u32[]{:S(2)}) copy-start(bf16[768,192]{0,1:T(8,128)(2,1)} %param.10) | copy-start | bytes 884740
  19.2 21.9 %copy-start.7 = (bf16[128,3072]{1,0:T(8,128)(2,1)}, bf16[128,3072]{1,0:T(8,128)(2,1)S(1)}, u32[]{:S(2)}) copy-start(bf16[128,3072]{1,0:T(8,128)(2,1)S(1)} %pad_maximum_fusion.refs_0_) | copy-start | bytes 2359300
  19.2 19.1 %collective-permute-start.1 = (bf16[128,3072]{1,0:T(8,128)(2,1)S(1)}, bf16[128,3072]{1,0:T(8,128)(2,1)S(1)}, u32[]{:S(2)}, u32[]{:S(2)}) collective-permute-start(bf16[128,3072]{1,0:T(8,128)(2,1)S(1)} %pad_maximum_fusion.refs_0_), channel_id=1, source_target_pairs={{0,4},{4,8},{8,12},{12,0},{1,5},{5,9},{9,13},{13,1},{2,6},{6,10},{... | collective-permute-start | bytes 2359304 | tf_op jit(solution)/shard_map/ppermute | solution.py:56
  21.2 17.2 %collective-permute-start.2 = (bf16[128,3072]{1,0:T(8,128)(2,1)S(1)}, bf16[128,3072]{1,0:T(8,128)(2,1)S(1)}, u32[]{:S(2)}, u32[]{:S(2)}) collective-permute-start(bf16[128,3072]{1,0:T(8,128)(2,1)S(1)} %pad_maximum_fusion.refs_0_), channel_id=1, source_target_pairs={{0,12},{4,0},{8,4},{12,8},{1,13},{5,1},{9,5},{13,9},{2,14},{6,2},{... | collective-permute-start | bytes 2359304 | tf_op jit(solution)/shard_map/ppermute | solution.py:56
  24.9 6.4 %collective-permute-start.3 = (bf16[192,768]{1,0:T(8,128)(2,1)S(1)}, bf16[192,768]{1,0:T(8,128)(2,1)S(1)}, u32[]{:S(2)}, u32[]{:S(2)}) collective-permute-start(bf16[192,768]{1,0:T(8,128)(2,1)S(1)} %fusion.5), channel_id=1, source_target_pairs={{0,128},{128,0},{1,129},{129,1},{2,130},{130,2},{3,131},{131,3},{4... | collective-permute-start | bytes 884744 | tf_op jit(solution)/shard_map/ppermute | solution.py:51
  38.3 2.7 %copy-start.10 = (bf16[128,3072]{1,0:T(8,128)(2,1)}, bf16[128,3072]{1,0:T(8,128)(2,1)S(1)}, u32[]{:S(2)}) copy-start(bf16[128,3072]{1,0:T(8,128)(2,1)S(1)} %collective-permute-done.1.refs_2_) | copy-start | bytes 2359300
  38.4 2.7 %copy-start.11 = (bf16[128,3072]{1,0:T(8,128)(2,1)}, bf16[128,3072]{1,0:T(8,128)(2,1)S(1)}, u32[]{:S(2)}) copy-start(bf16[128,3072]{1,0:T(8,128)(2,1)S(1)} %collective-permute-done.2.refs_4_) | copy-start | bytes 2359300
  41.1 51.8 %all-to-all-start = ((bf16[16,136,768]{2,1,0:T(8,128)(2,1)}), bf16[16,136,768]{2,1,0:T(8,128)(2,1)S(1)}, u32[]{:S(2)}, u32[]{:S(2)}) async-start(bf16[16,136,768]{2,1,0:T(8,128)(2,1)} %split_columns.1), calls=%async_computation | async-start | bytes 6684672 | tf_op jit(solution)/shard_map/all_to_all | solution.py:339
  50.6 127.7 %reduce-scatter.2.cloned.1.call-start = ((), (), s32[]{:S(2)}) async-start(), calls=%async_computation.4 | async-start | bytes 5308416 | tf_op jit(solution)/shard_map/reduce_scatter | solution.py:347
  50.7 50.2 %collective-permute-start.4 = (bf16[128,3072]{1,0:T(8,128)(2,1)}, bf16[128,3072]{1,0:T(8,128)(2,1)}, u32[]{:S(2)}, u32[]{:S(2)}) collective-permute-start(bf16[128,3072]{1,0:T(8,128)(2,1)} %copy-done.7), channel_id=1, source_target_pairs={{0,1},{1,0},{2,3},{3,2},{4,5},{5,4},{6,7},{7,6},{8,9},{9,8},{10,11... | collective-permute-start | bytes 2359304 | tf_op jit(solution)/shard_map/ppermute | solution.py:51
  50.9 48.7 %collective-permute-start.7 = (bf16[64,3072]{1,0:T(8,128)(2,1)}, bf16[64,3072]{1,0:T(8,128)(2,1)}, u32[]{:S(2)}, u32[]{:S(2)}) collective-permute-start(bf16[64,3072]{1,0:T(8,128)(2,1)} %slice.36), channel_id=1, source_target_pairs={{0,4},{4,8},{8,12},{12,0},{1,5},{5,9},{9,13},{13,1},{2,6},{6,10},{... | collective-permute-start | bytes 1179656 | tf_op jit(solution)/shard_map/ppermute | solution.py:56
  52.5 47.1 %collective-permute-start.8 = (bf16[64,3072]{1,0:T(8,128)(2,1)}, bf16[64,3072]{1,0:T(8,128)(2,1)}, u32[]{:S(2)}, u32[]{:S(2)}) collective-permute-start(bf16[64,3072]{1,0:T(8,128)(2,1)} %slice.37), channel_id=1, source_target_pairs={{0,12},{4,0},{8,4},{12,8},{1,13},{5,1},{9,5},{13,9},{2,14},{6,2},{... | collective-permute-start | bytes 1179656 | tf_op jit(solution)/shard_map/ppermute | solution.py:56
  53.7 47.1 %collective-permute-start.5 = (bf16[128,3072]{1,0:T(8,128)(2,1)}, bf16[128,3072]{1,0:T(8,128)(2,1)}, u32[]{:S(2)}, u32[]{:S(2)}) collective-permute-start(bf16[128,3072]{1,0:T(8,128)(2,1)} %copy-done.10), channel_id=1, source_target_pairs={{0,1},{1,0},{2,3},{3,2},{4,5},{5,4},{6,7},{7,6},{8,9},{9,8},{10,11... | collective-permute-start | bytes 2359304 | tf_op jit(solution)/shard_map/ppermute | solution.py:51
  54.5 46.3 %collective-permute-start.6 = (bf16[128,3072]{1,0:T(8,128)(2,1)}, bf16[128,3072]{1,0:T(8,128)(2,1)}, u32[]{:S(2)}, u32[]{:S(2)}) collective-permute-start(bf16[128,3072]{1,0:T(8,128)(2,1)} %copy-done.11), channel_id=1, source_target_pairs={{0,1},{1,0},{2,3},{3,2},{4,5},{5,4},{6,7},{7,6},{8,9},{9,8},{10,11... | collective-permute-start | bytes 2359304 | tf_op jit(solution)/shard_map/ppermute | solution.py:51
  97.3 1.1 copy-start.2
  98.5 1.2 copy-start.3
  99.6 2.5 %collective-permute-start.10 = (bf16[64,3072]{1,0:T(8,128)(2,1)}, bf16[64,3072]{1,0:T(8,128)(2,1)S(1)}, u32[]{:S(2)}, u32[]{:S(2)}) collective-permute-start(bf16[64,3072]{1,0:T(8,128)(2,1)} %collective-permute-done.8.refs_7_), channel_id=1, source_target_pairs={{0,1},{1,0},{2,3},{3,2},{4,5},{5,4},{6,7},{7,6},{8,9},{9,8},{10,11... | collective-permute-start | bytes 1179656 | tf_op jit(solution)/shard_map/ppermute | solution.py:51
  100.6 2.1 collective-permute-start.9
  102.1 9.9 %copy-start = (bf16[64,3072]{1,0:T(8,128)(2,1)}, bf16[64,3072]{1,0:T(8,128)(2,1)S(1)}, u32[]{:S(2)}) copy-start(bf16[64,3072]{1,0:T(8,128)(2,1)S(1)} %collective-permute-done.10.refs_9_) | copy-start | bytes 1179652
  102.7 9.4 %copy-start.1 = (bf16[64,3072]{1,0:T(8,128)(2,1)}, bf16[64,3072]{1,0:T(8,128)(2,1)S(1)}, u32[]{:S(2)}) copy-start(bf16[64,3072]{1,0:T(8,128)(2,1)S(1)} %collective-permute-done.9.refs_8_) | copy-start | bytes 1179652
  112.1 1.0 copy-start.6
  116.4 26.2 %copy-start.4 = (f32[192,768]{1,0:T(8,128)}, f32[192,768]{1,0:T(8,128)S(1)}, u32[]{:S(2)}) copy-start(f32[192,768]{1,0:T(8,128)S(1)} %get-tuple-element.46) | copy-start | bytes 1769476
  116.4 14.5 %collective-permute-start.11 = (f32[192,768]{1,0:T(8,128)S(1)}, f32[192,768]{1,0:T(8,128)S(1)}, u32[]{:S(2)}, u32[]{:S(2)}) collective-permute-start(f32[192,768]{1,0:T(8,128)S(1)} %get-tuple-element.46), channel_id=1, source_target_pairs={{0,128},{128,0},{1,129},{129,1},{2,130},{130,2},{3,131},{131,3},{4... | collective-permute-start | bytes 1769480 | tf_op jit(solution)/shard_map/ppermute | solution.py:51
  131.0 11.7 %copy-start.8 = (f32[192,768]{1,0:T(8,128)}, f32[192,768]{1,0:T(8,128)S(1)}, u32[]{:S(2)}) copy-start(f32[192,768]{1,0:T(8,128)S(1)} %collective-permute-done.11) | copy-start | bytes 1769476
  149.7 51.4 %all-to-all-start.1 = ((bf16[16,128,768]{2,1,0:T(8,128)(2,1)}), bf16[16,128,768]{2,1,0:T(8,128)(2,1)S(1)}, u32[]{:S(2)}, u32[]{:S(2)}) async-start(bf16[16,128,768]{2,1,0:T(8,128)(2,1)} %unpack.1), calls=%async_computation.1 | async-start | bytes 6291456 | tf_op jit(solution)/shard_map/all_to_all | solution.py:351
  180.0 38.5 %collective-permute-start.12 = (bf16[192,768]{1,0:T(8,128)(2,1)S(1)}, bf16[192,768]{1,0:T(8,128)(2,1)}, u32[]{:S(2)}, u32[]{:S(2)}) collective-permute-start(bf16[192,768]{1,0:T(8,128)(2,1)S(1)} %get-tuple-element.52), channel_id=1, source_target_pairs={{0,128},{128,0},{1,129},{129,1},{2,130},{130,2},{3,131},{131,3},{4... | collective-permute-start | bytes 884744 | tf_op jit(solution)/shard_map/ppermute | solution.py:51
  201.7 16.8 %all-to-all-start.2 = ((f32[32,1,192]{2,1,0:T(1,128)}), f32[32,1,192]{2,1,0:T(1,128)S(1)}, u32[]{:S(2)}, u32[]{:S(2)}) async-start(f32[32,1,192]{2,1,0:T(1,128)} %all_to_all.16), calls=%async_computation.3 | async-start | bytes 65536 | tf_op jit(solution)/shard_map/all_to_all | solution.py:360
Sparse Core Ops, SparseCore 0:
  39.6 64.6 all-gather.2
  112.2 66.0 reduce-scatter.1
